TPU v7x, 256 devices: a whole 4x4x8 slice. The times are simulated.
256 devices in a mesh: grp: 16 (over x, z_lo, core), row: 4 (over z_hi), col: 4 (over y).
Axes of the slice: x: 4, y: 4, z: 8 (z_hi: 4, z_lo: 2; z = z_hi * 2 + z_lo), core: 2. Of those that a mesh axis runs over, the one named last changes fastest.
Arguments:
- volume: float32 [32, 32, 32, 512], P(None, 'grp', 'row', 'col'), may hold values from -6 to 6
- forcing: float32 [32, 32, 32, 512], P(None, 'grp', 'row', 'col'), may hold values from -6 to 6
- medium: float32 [2, 32, 32, 512], P(None, 'grp', 'row', 'col'), may hold values from 0.5 to 3
- points: float32 [3, 32768], P(None, ('grp', 'row', 'col')), may hold values from 0 to 4
- weights: float32 [32768], P(('grp', 'row', 'col')), may hold values from 0.05 to 0.5
- cell_map: int32 [32768], P(('grp', 'row', 'col')), may hold values from 0 to 2047
- near_list: int32 [256, 256], replicated, may hold values from 0 to 1, as said below
Outputs:
- new_volume: float32 [32, 32, 32, 512], P(None, 'grp', 'row', 'col')
- potential: float32 [32, 32768], P(None, ('grp', 'row', 'col'))
Inputs may be any that keep to these rules, and one draw needn't show every extreme that they name: cell_map[p] numbers a cell of tile p // 128 in row-major order of the tile's 2 x 8 x 128 cells. near_list[i, j] = 1 lists cluster j as near to cluster i; every cluster lists itself, and how many clusters a cluster lists differs from cluster to cluster.
All inputs are finite; a program needn't handle non-finite values.
Results may differ from a plain program's by a relative error of at most 0.0041.
Values may be sent and summed in bfloat16 or wider, within the bound.
No kernel may reach another device: no remote copies, remote signals or barrier semaphores. Data moves between devices by JAX's collectives and lax.ppermute only.
A program may use at most 64 MiB of HBM per device.

v0:
```python
import math

import jax
import jax.numpy as jnp
import numpy as np
from jax import lax
from jax.experimental import pallas as pl
from jax.experimental.pallas import tpu as pltpu
from jax.sharding import Mesh
from jax.sharding import PartitionSpec as P

RHS = 16
CX = 2
CY = 8
CZ = 128
CH = 32
PTS = 128

FOUR_PI = 4.0 * 3.141592653589793
WAVENUMBER = 10.0
SOFTENING = 0.01
RELAX_RATE = 0.8
COUPLING = 0.5

TURN = WAVENUMBER / (2.0 * 3.141592653589793)
CENTRE = 2.0
SCALE = TURN / FOUR_PI

AXES = ("x", "zl", "core", "zh", "y")
SIZES = dict(x=4, zl=2, core=2, zh=4, y=4)
STRIDES = dict(x=64, zl=32, core=16, zh=4, y=1)
ALPHA = ("x", "core", "y")
BETA = ("zl", "zh")
NA = math.prod(SIZES[a] for a in ALPHA)
NB = math.prod(SIZES[a] for a in BETA)
TILES = NA * NB
ROW = 64
EXT = 32
USED = 24
STRIPS = CH * CX * CY // CZ
NT = 4
LIST = 384

f32, bf16, i32 = jnp.float32, jnp.bfloat16, jnp.int32


def sine_coefficients():
    f = np.cos(np.linspace(0, np.pi / 2, 4001)) * 0.5 + 1e-9
    z = f * f
    y = np.sin(np.pi / 2 * f) / f
    basis = np.stack([np.ones_like(z), z, z * z], 1)
    weight = np.ones_like(f)
    fit = None
    for _ in range(300):
        fit, *_ = np.linalg.lstsq(basis * (weight * f)[:, None], y * weight * f, rcond=None)
        err = np.abs((basis @ fit - y) * f)
        weight = weight * (1e-12 + err / err.max()) ** 0.3
        weight = weight / weight.max()
    return [float(c) for c in fit]


SIN = sine_coefficients()
LAM2 = 2.0 * math.sqrt(2.0)
LAM = math.sqrt(LAM2)
RT2 = math.sqrt(2.0)
S0, S1, S2 = [c * LAM for c in SIN]


def dot(a, b, dims):
    return lax.dot_general(a, b, (dims, ((), ())), preferred_element_type=f32)


def split3(x):
    hi = x.astype(bf16).astype(f32)
    rest = x - hi
    mid = rest.astype(bf16).astype(f32)
    return hi, mid, rest - mid


def cluster_of(index, axes):
    total = 0
    for axis in reversed(axes):
        total = total + (index % SIZES[axis]) * STRIDES[axis]
        index = index // SIZES[axis]
    return total


def own_part(axes):
    total = 0
    for axis in axes:
        total = total + lax.axis_index(axis) * STRIDES[axis]
    return total


def iota(shape, dim):
    return lax.broadcasted_iota(i32, shape, dim)


def mask(condition):
    return condition.astype(f32).astype(bf16)


def point_rows(pts, ends, scr, src_ref, tgt_ref):
    p = (pts - CENTRE) * TURN
    r = jnp.sum(p * p, axis=0, keepdims=True)
    ah, am, al = split3(-2.0 * p)
    bh, bm, bl = split3(p)
    sh, sm, sl = split3(r)
    th, tm, tl = split3(r + SOFTENING * TURN * TURN)
    one = jnp.ones((1, PTS), f32)
    scr[...] = jnp.zeros((EXT, PTS), f32)

    def fill(*groups):
        for n, (three, last) in enumerate(groups):
            scr[4 * n : 4 * n + 3, :] = three
            scr[4 * n + 3 : 4 * n + 4, :] = last

    fill((ah, sh), (ah, one), (am, sm), (am, one), (ah, sl), (al, one))
    src_ref[...] = scr[...].astype(bf16)
    fill((bh, one), (bm, th), (bh, one), (bm, tm), (bl, one), (bh, tl))
    for k in range(STRIPS):
        for end in range(2):
            scr[USED + STRIPS * end + k : USED + STRIPS * end + k + 1, :] = ends[end : end + 1, CZ * k : CZ * (k + 1)]
    tgt_ref[...] = jnp.broadcast_to(scr[...].astype(bf16)[None], tgt_ref.shape)


def tile_order(near, order_ref):
    pick_rows = mask(iota((NA, 256), 1) == cluster_of(iota((NA, 256), 0), ALPHA) + own_part(BETA))
    wide = iota((256, PTS), 1)
    pick_cols = mask((iota((256, PTS), 0) == cluster_of(wide, BETA) + own_part(ALPHA)) & (wide < NB))
    listed = dot(dot(pick_rows, near, ((1,), (0,))).astype(bf16), pick_cols, ((1,), (0,))).astype(bf16)
    k = iota((PTS, TILES), 1)
    flat = dot(listed, mask(iota((PTS, TILES), 0) == k % NB), ((1,), (0,)))
    own = iota((NA, TILES), 1) // NB == iota((NA, TILES), 0)
    flat = jnp.sum(jnp.where(own, flat, 0.0), axis=0, keepdims=True)
    square = (TILES, TILES)
    before = mask(iota(square, 0) < iota(square, 1))
    place = dot(jnp.broadcast_to(flat, (8, TILES)).astype(bf16), before, ((1,), (0,)))[0:1]
    hit = mask((place.astype(i32) == iota(square, 0)) & (flat > 0.5))
    k = iota((8, TILES), 1)
    row = iota((8, TILES), 0)
    codes = jnp.where(row == 0, k // NB, jnp.where(row == 1, k % NB, 0)).astype(f32).astype(bf16)
    found = dot(codes, hit, ((1,), (1,))).astype(i32)
    count = jnp.sum(flat, axis=1, keepdims=True).astype(i32)
    entry = jnp.where(iota((1, TILES), 1) < count, found[0:1] * ROW + found[1:2], NB)
    order_ref[...] = jnp.full((8, LIST), NB, i32)
    order_ref[0:1, 0:TILES] = entry
    order_ref[1:2, 0:PTS] = jnp.broadcast_to(count, (1, PTS))


def parities():
    return lax.axis_index("core") % 2, lax.axis_index("zh") % 2


def prep_kernel(vol_ref, pts_ref, near_ref, tgt_ref, src_ref, order_ref, xe_ref, xo_ref, ye_ref, yo_ref, scr):
    v = vol_ref[...].reshape(CH * CX * CY, CZ).astype(bf16)
    row, col = iota((16, CZ), 0), iota((16, CZ), 1)
    pick = mask(((row == 0) & (col == CZ - 1)) | ((row == 1) & (col == 0)))
    point_rows(pts_ref[...], dot(pick, v, ((1,), (1,))), scr, src_ref, tgt_ref)
    px, py = parities()
    xe_ref[...] = vol_ref[:, 1 - px].astype(bf16)
    xo_ref[...] = vol_ref[:, px].astype(bf16)
    low = vol_ref[:, :, 0, :].reshape(CH * CX, CZ).astype(bf16)
    high = vol_ref[:, :, CY - 1, :].reshape(CH * CX, CZ).astype(bf16)
    ye_ref[...] = jnp.where(py == 0, high, low)
    yo_ref[...] = jnp.where(py == 0, low, high)
    tile_order(mask(near_ref[...] != 0), order_ref)


def joint_index(axes):
    total = 0
    for axis in axes:
        total = total * SIZES[axis] + lax.axis_index(axis)
    return total


def relax_kernel(vol_ref, forc_ref, med_ref, xe_ref, xo_ref, ye_ref, yo_ref, tgt_ref,
                 wts_ref, map_ref, src_ref, rel_ref, pack_ref, ends):
    px, py = parities()
    v = vol_ref[...]
    xe, xo = xe_ref[...].astype(f32), xo_ref[...].astype(f32)
    xl, xh = jnp.where(px == 0, xo, xe), jnp.where(px == 0, xe, xo)
    bx = jnp.stack([xl + v[:, 1], v[:, 0] + xh], axis=1)
    v3 = v.reshape(CH * CX, CY, CZ)
    row = iota(v3.shape, 1)
    ye, yo = ye_ref[...].astype(f32), yo_ref[...].astype(f32)
    yl, yh = jnp.where(py == 0, yo, ye)[:, None, :], jnp.where(py == 0, ye, yo)[:, None, :]
    by = jnp.where(row == 0, yl, pltpu.roll(v3, 1, 1)) + jnp.where(row == CY - 1, yh, pltpu.roll(v3, CY - 1, 1))
    v2 = v.reshape(CH * CX * CY, CZ)
    lane = iota(v2.shape, 1)
    row, col = iota((16, CZ), 0), iota((16, CZ), 1)
    place = mask(((row == 0) & (col == 0)) | ((row == 1) & (col == CZ - 1)))
    own, along = joint_index(ALPHA), lax.axis_index("y")
    half = EXT // 2
    before = tgt_ref[jnp.maximum(own - 1, 0), half:, :].astype(f32) * (along > 0).astype(f32)
    after = tgt_ref[jnp.minimum(own + 1, NA - 1), half:, :].astype(f32) * (along < SIZES["y"] - 1).astype(f32)
    ends[...] = jnp.zeros_like(ends)
    for k in range(STRIPS):
        spot = USED - half + k
        ends[0:1, CZ * k : CZ * (k + 1)] = before[spot : spot + 1]
        ends[1:2, CZ * k : CZ * (k + 1)] = after[spot + STRIPS : spot + STRIPS + 1]
    zhalo = ends[...].astype(bf16)
    bz = (
        jnp.where(lane == 0, 0.0, pltpu.roll(v2, 1, 1))
        + jnp.where(lane == CZ - 1, 0.0, pltpu.roll(v2, CZ - 1, 1))
        + dot(zhalo, place, ((0,), (0,)))
    )
    beside = bx + by.reshape(v.shape) + bz.reshape(v.shape)
    a = med_ref[0]
    b = med_ref[1]
    lap = 6.0 * v - beside
    re, im = v[:RHS], v[RHS:]
    out_re = lap[:RHS] - a[None] * re + b[None] * im
    out_im = lap[RHS:] - a[None] * im - b[None] * re
    res = forc_ref[...] - jnp.concatenate([out_re, out_im], 0)
    rate = RELAX_RATE / (6.0 - a)
    relaxed = v + res * rate[None]
    rel_ref[...] = relaxed
    cells = map_ref[...]
    pick = mask(iota((CZ, PTS), 0) == cells % CZ)
    hi, mid, lo = split3(relaxed.reshape(CH * CX * CY, CZ))
    at = (
        dot(hi.astype(bf16), pick, ((1,), (0,)))
        + dot(mid.astype(bf16), pick, ((1,), (0,)))
        + dot(lo.astype(bf16), pick, ((1,), (0,)))
    )
    keep = (iota((CX * CY, PTS), 0) == cells // CZ).astype(f32)
    at = at.reshape(CH, CX * CY, PTS) * keep[None]
    traces = (jnp.sum(at, axis=1) * wts_ref[...]).astype(bf16)
    pack_ref[:, 0:EXT, :] = jnp.broadcast_to(src_ref[...][None], (NB, EXT, PTS))
    pack_ref[:, EXT:, :] = jnp.broadcast_to(traces[None], (NB, CH, PTS))


def evaluate(dist2):
    inv = lax.rsqrt(dist2)
    turns = dist2 * inv
    f = turns - jnp.round(turns)
    z = f * f
    s = f * ((S2 * z + S1) * z + S0)
    a = s * s
    c2 = RT2 - a
    w = LAM2 - a
    c = w * lax.rsqrt(w)
    s2 = s * c
    over = SCALE * inv
    e = s2 * over
    return (over - e * s2).astype(bf16), (e * c2).astype(bf16)


def pair_kernel(order_ref, pack_ref, tgt_ref, out_ref, sum_ref, a_ref, w_ref, d0, d1, g0, g1):
    sum_ref[...] = jnp.zeros_like(sum_ref)
    for j in range(NB):
        a_ref[j] = jnp.transpose(pack_ref[j, 0:EXT, :].astype(f32)).astype(bf16)
        t = pack_ref[j, EXT:, :]
        w_ref[j, :, 0:PTS] = t
        w_ref[j, :, PTS:] = jnp.concatenate([-t[RHS:], t[:RHS]], 0)
    a_ref[NB] = a_ref[0]
    w_ref[NB] = jnp.zeros((CH, 2 * PTS), bf16)
    pairs = (order_ref[1, 0] + (2 * NT - 1)) // (2 * NT)

    def code(group, q):
        c = order_ref[0, group * NT + q]
        return c // ROW, c % ROW

    def dist(group, d_ref):
        for q in range(NT):
            i, j = code(group, q)
            d_ref[q] = jnp.dot(a_ref[j], tgt_ref[i], preferred_element_type=f32)

    def add(group, g_ref):
        for q in range(NT):
            i, j = code(group, q)
            sum_ref[i] += jnp.dot(w_ref[j], g_ref[q], preferred_element_type=f32)

    def values(d_ref, g_ref):
        for q in range(NT):
            re, im = evaluate(d_ref[q])
            g_ref[q, 0:PTS, :] = re
            g_ref[q, PTS:, :] = im

    dist(0, d0)
    g1[...] = jnp.zeros_like(g1)

    def body(k, _):
        dist(2 * k + 1, d1)
        values(d0, g0)
        add(jnp.maximum(2 * k - 1, 0), g1)
        dist(2 * k + 2, d0)
        values(d1, g1)
        add(2 * k, g0)
        return 0

    lax.fori_loop(0, pairs, body, 0)
    add(jnp.maximum(2 * pairs - 1, 0), g1)
    out_ref[...] = sum_ref[...].astype(bf16)


def finish_kernel(part_ref, rel_ref, map_ref, new_ref, pot_ref):
    pot = jnp.sum(part_ref[...].astype(f32), axis=0)
    pot_ref[...] = pot
    cells = map_ref[...]
    keep = (iota((CX * CY, PTS), 0) == cells // CZ).astype(f32)
    pick = mask(iota((CZ, PTS), 0) == cells % CZ)
    spread = jnp.zeros((CH * CX * CY, CZ), f32)
    for part in split3(pot * COUPLING):
        wide = (part[:, None, :] * keep[None]).reshape(CH * CX * CY, PTS).astype(bf16)
        spread = spread + dot(wide, pick, ((1,), (1,)))
    new_ref[...] = rel_ref[...] + spread.reshape(CH, CX, CY, CZ)


def call(kernel, name, args, spaces, outs, scratch=(), keep=True):
    args = [a if c == "s" else pltpu.with_memory_space_constraint(a, pltpu.VMEM) for a, c in zip(args, spaces)]
    shaped = pltpu.VMEM if keep else jax.ShapeDtypeStruct
    return pl.pallas_call(
        kernel,
        out_shape=[shaped(shape, dtype) for shape, dtype in outs],
        in_specs=[pl.BlockSpec(memory_space=pltpu.SMEM if c == "s" else pltpu.VMEM) for c in spaces],
        out_specs=[pl.BlockSpec(memory_space=pltpu.VMEM)] * len(outs),
        scratch_shapes=[pltpu.VMEM(shape, dtype) for shape, dtype in scratch],
        name=name,
    )(*args)


def swap(x, axes, parity):
    size = math.prod(SIZES[a] for a in axes)
    pairs = [q for k in range(parity, size - 1, 2) for q in ((k, k + 1), (k + 1, k))]
    return lax.ppermute(x, axes if len(axes) > 1 else axes[0], pairs)


def on_device(volume, forcing, medium, points, weights, cell_map, near_list):
    cells = cell_map[None, :]
    face_x, face_y = (CH, CY, CZ), (CH * CX, CZ)
    tgt, src, order, xe, xo, ye, yo = call(
        prep_kernel,
        "prep",
        (volume, points, near_list),
        "vvv",
        [((NA, EXT, PTS), bf16), ((EXT, PTS), bf16), ((8, LIST), i32)]
        + [(face, bf16) for face in (face_x, face_x, face_y, face_y)],
        [((EXT, PTS), f32)],
    )
    targets = lax.all_to_all(tgt, ALPHA, 0, 0, tiled=True)
    grp = ("x", "zl", "core")
    ye, yo = swap(ye, ("zh",), 0), swap(yo, ("zh",), 1)
    xo, xe = swap(xo, grp, 1), swap(xe, grp, 0)
    relaxed, pack = call(
        relax_kernel,
        "relax",
        (volume, forcing, medium, xe, xo, ye, yo, targets, weights[None, :], cells, src),
        "v" * 11,
        [((CH, CX, CY, CZ), f32), ((NB, EXT + CH, PTS), bf16)],
        [((16, CH * CX * CY), f32)],
    )
    packs = lax.all_to_all(pack, BETA, 0, 0, tiled=True)
    (part,) = call(
        pair_kernel,
        "pairs",
        (order, packs, targets),
        "svv",
        [((NA, CH, PTS), bf16)],
        [
            ((NA, CH, PTS), f32),
            ((NB + 1, PTS, EXT), bf16),
            ((NB + 1, CH, 2 * PTS), bf16),
            ((NT, PTS, PTS), f32),
            ((NT, PTS, PTS), f32),
            ((NT, 2 * PTS, PTS), bf16),
            ((NT, 2 * PTS, PTS), bf16),
        ],
    )
    parts = lax.all_to_all(part, ALPHA, 0, 0, tiled=True)
    new_volume, potential = call(
        finish_kernel,
        "finish",
        (parts, relaxed, cells),
        "vvv",
        [((CH, CX, CY, CZ), f32), ((CH, PTS), f32)],
        keep=False,
    )
    return new_volume, potential


def solution(mesh):
    split = Mesh(np.asarray(mesh.devices).reshape([SIZES[a] for a in AXES]), AXES)
    grid = P(None, ("x", "zl", "core"), "zh", "y")
    return jax.shard_map(
        on_device,
        mesh=split,
        in_specs=(grid, grid, grid, P(None, AXES), P(AXES), P(AXES), P()),
        out_specs=(grid, P(None, AXES)),
        check_vma=False,
    )
```

profile of v0, /device:TPU:1, one launch (start us, length us, event | category | flops | bytes accessed | tf_op | source)
XLA Modules:
  0.0 71.3 jit_solution(1891394837384192912)
XLA Ops:
  0.6 0.0 copy-start
  0.6 0.9 %copy-done = f32[32,2,8,128]{3,2,1,0:T(8,128)S(1)} copy-done((f32[32,2,8,128]{3,2,1,0:T(8,128)S(1)}, f32[32,2,8,128]{3,2,1,0:T(8,128)}, u32[]{:S(2)}) %copy-start) | copy-done | bytes 262168
  1.6 0.0 copy-start.2
  1.6 0.9 %copy-done.2 = s32[256,256]{1,0:T(8,128)S(1)} copy-done((s32[256,256]{1,0:T(8,128)S(1)}, s32[256,256]{1,0:T(8,128)}, u32[]{:S(2)}) %copy-start.2) | copy-done | bytes 262168
  2.5 0.0 copy-start.5
  2.5 0.7 copy-done.5
  3.2 1.1 %prep.1 = (bf16[32,32,128]{2,1,0:T(8,128)(2,1)}, bf16[32,128]{1,0:T(8,128)(2,1)S(1)}, s32[8,384]{1,0:T(8,128)S(1)}, bf16[32,8,128]{2,1,0:T(8,128)(2,1)S(1)}, bf1...) custom-call(f32[32,2,8,128]{3,2,1,0:T(8,128)S(1)} %copy-done, ...), custom_call_target="tpu_custom_call" | custom-call | tf_op jit(solution)/shard_map/prep/pallas_call | solution.py:314
  4.3 0.0 copy-start.4
  4.3 0.0 copy-start.1
  4.3 0.0 copy-start.3
  4.3 0.6 copy-done.4
  4.9 8.6 %all-to-all-start = ((bf16[32,32,128]{2,1,0:T(8,128)(2,1)}), bf16[32,32,128]{2,1,0:T(8,128)(2,1)S(1)}, u32[]{:S(2)}, u32[]{:S(2)}) async-start(bf16[32,32,128]{2,1,0:T(8,128)(2,1)} %get-tuple-element.16), calls=%async_computation | async-start | bytes 524288 | tf_op jit(solution)/shard_map/all_to_all | solution.py:342
  13.5 0.3 collective-permute-start
  13.8 3.7 %collective-permute-start.1 = (bf16[32,8,128]{2,1,0:T(8,128)(2,1)S(1)}, bf16[32,8,128]{2,1,0:T(8,128)(2,1)S(1)}, u32[]{:S(2)}, u32[]{:S(2)}) collective-permute-start(bf16[32,8,128]{2,1,0:T(8,128)(2,1)S(1)} %get-tuple-element.13), channel_id=1, source_target_pairs={{16,32},{32,16},{48,64},{64,48},{80,96},{96,80},{112,128},{128,112... | collective-permute-start | bytes 196616 | tf_op jit(solution)/shard_map/ppermute | solution.py:327
  17.5 3.1 %collective-permute-start.2 = (bf16[64,128]{1,0:T(8,128)(2,1)S(1)}, bf16[64,128]{1,0:T(8,128)(2,1)S(1)}, u32[]{:S(2)}, u32[]{:S(2)}) collective-permute-start(bf16[64,128]{1,0:T(8,128)(2,1)S(1)} %get-tuple-element.14), channel_id=1, source_target_pairs={{0,4},{4,0},{8,12},{12,8},{1,5},{5,1},{9,13},{13,9},{2,6},{6,2},{1... | collective-permute-start | bytes 49160 | tf_op jit(solution)/shard_map/ppermute | solution.py:327
  20.6 0.7 collective-permute-start.3
  21.2 0.8 %collective-permute-done.2.ye_ref = bf16[64,128]{1,0:T(8,128)(2,1)S(1)} collective-permute-done((bf16[64,128]{1,0:T(8,128)(2,1)S(1)}, bf16[64,128]{1,0:T(8,128)(2,1)S(1)}, u32[]{:S(2)}, u32[]{:S(2)}) %collective-permute-start.2) | collective-permute-done | bytes 16416 | tf_op jit(solution)/shard_map/ppermute | solution.py:327
  22.0 0.0 collective-permute-done.3.yo_ref
  22.0 0.0 collective-permute-done.xe_ref
  22.0 0.0 collective-permute-done.1.xo_ref
  22.0 0.3 all-to-all-done.tgt_ref
  22.3 0.0 copy-start.6
  22.3 0.0 copy-start.7
  22.3 0.0 copy-done.1
  22.3 0.0 copy-done.3
  22.3 0.6 copy-done.6
  22.9 0.0 copy-done.7
  23.0 0.6 relax.1
  23.6 18.1 %all_to_all.15.pack_ref = bf16[8,64,128]{2,1,0:T(8,128)(2,1)S(1)} all-to-all(bf16[8,64,128]{2,1,0:T(8,128)(2,1)S(1)} %get-tuple-element.18), channel_id=1, replica_groups=mesh['x'=4,'zl'=2,'core'=2,'zh'=4,'y'=4] {'zl','zh'}, dimensions={0} | all-to-all | bytes 262144 | tf_op jit(solution)/shard_map/all_to_all | solution.py:354
  41.7 10.8 %pairs.1 = bf16[32,32,128]{2,1,0:T(8,128)(2,1)S(1)} custom-call(s32[8,384]{1,0:T(8,128)} %copy-done.4, bf16[8,64,128]{2,1,0:T(8,128)(2,1)S(1)} %all_to_all.15.pack_ref, bf16[32,32,128]{2,1,0:T(8,128)(2,1)S(1)} %all-to-all-done.tgt_ref), custom_call_target="tpu_custom_call" | custom-call | tf_op jit(solution)/shard_map/pairs/pallas_call | solution.py:314
  52.6 17.7 %all_to_all.16.part_ref = bf16[32,32,128]{2,1,0:T(8,128)(2,1)S(1)} all-to-all(bf16[32,32,128]{2,1,0:T(8,128)(2,1)S(1)} %pairs.1), channel_id=1, replica_groups=mesh['x'=4,'zl'=2,'core'=2,'zh'=4,'y'=4] {'x','core','y'}, dimensions={0} | all-to-all | bytes 524288 | tf_op jit(solution)/shard_map/all_to_all | solution.py:371
  70.3 1.0 %finish.1 = (f32[32,2,8,128]{3,2,1,0:T(8,128)}, f32[32,128]{1,0:T(8,128)}) custom-call(bf16[32,32,128]{2,1,0:T(8,128)(2,1)S(1)} %all_to_all.16.part_ref, f32[32,2,8,128]{3,2,1,0:T(8,128)S(1)} %get-tuple-element.19.rel_ref, s32[1,128]{1,0:T(1,128)S(1)} %bitcast.3), custom_call_target="tpu_custom_call" | custom-call | tf_op jit(solution)/shard_map/finish/pallas_call | solution.py:314
Async XLA Ops:
  0.6 1.0 %copy-start = (f32[32,2,8,128]{3,2,1,0:T(8,128)S(1)}, f32[32,2,8,128]{3,2,1,0:T(8,128)}, u32[]{:S(2)}) copy-start(f32[32,2,8,128]{3,2,1,0:T(8,128)} %vol_ref.3) | copy-start | bytes 786436
  1.6 0.9 %copy-start.2 = (s32[256,256]{1,0:T(8,128)S(1)}, s32[256,256]{1,0:T(8,128)}, u32[]{:S(2)}) copy-start(s32[256,256]{1,0:T(8,128)} %near_ref.1) | copy-start | bytes 786436
  2.5 0.7 copy-start.5
  4.3 0.6 copy-start.4
  4.3 18.0 %copy-start.1 = (f32[32,2,8,128]{3,2,1,0:T(8,128)S(1)}, f32[32,2,8,128]{3,2,1,0:T(8,128)}, u32[]{:S(2)}) copy-start(f32[32,2,8,128]{3,2,1,0:T(8,128)} %forc_ref.1) | copy-start | bytes 786436
  4.3 18.0 %copy-start.3 = (f32[2,2,8,128]{3,2,1,0:T(8,128)S(1)}, f32[2,2,8,128]{3,2,1,0:T(8,128)}, u32[]{:S(2)}) copy-start(f32[2,2,8,128]{3,2,1,0:T(8,128)} %med_ref.1) | copy-start | bytes 49156
  4.9 17.4 %all-to-all-start = ((bf16[32,32,128]{2,1,0:T(8,128)(2,1)}), bf16[32,32,128]{2,1,0:T(8,128)(2,1)S(1)}, u32[]{:S(2)}, u32[]{:S(2)}) async-start(bf16[32,32,128]{2,1,0:T(8,128)(2,1)} %get-tuple-element.16), calls=%async_computation | async-start | bytes 524288 | tf_op jit(solution)/shard_map/all_to_all | solution.py:342
  13.5 8.5 %collective-permute-start = (bf16[32,8,128]{2,1,0:T(8,128)(2,1)S(1)}, bf16[32,8,128]{2,1,0:T(8,128)(2,1)S(1)}, u32[]{:S(2)}, u32[]{:S(2)}) collective-permute-start(bf16[32,8,128]{2,1,0:T(8,128)(2,1)S(1)} %get-tuple-element.12), channel_id=1, source_target_pairs={{0,16},{16,0},{32,48},{48,32},{64,80},{80,64},{96,112},{112,96},{1... | collective-permute-start | bytes 196616 | tf_op jit(solution)/shard_map/ppermute | solution.py:327
  13.8 8.2 %collective-permute-start.1 = (bf16[32,8,128]{2,1,0:T(8,128)(2,1)S(1)}, bf16[32,8,128]{2,1,0:T(8,128)(2,1)S(1)}, u32[]{:S(2)}, u32[]{:S(2)}) collective-permute-start(bf16[32,8,128]{2,1,0:T(8,128)(2,1)S(1)} %get-tuple-element.13), channel_id=1, source_target_pairs={{16,32},{32,16},{48,64},{64,48},{80,96},{96,80},{112,128},{128,112... | collective-permute-start | bytes 196616 | tf_op jit(solution)/shard_map/ppermute | solution.py:327
  17.5 4.5 %collective-permute-start.2 = (bf16[64,128]{1,0:T(8,128)(2,1)S(1)}, bf16[64,128]{1,0:T(8,128)(2,1)S(1)}, u32[]{:S(2)}, u32[]{:S(2)}) collective-permute-start(bf16[64,128]{1,0:T(8,128)(2,1)S(1)} %get-tuple-element.14), channel_id=1, source_target_pairs={{0,4},{4,0},{8,12},{12,8},{1,5},{5,1},{9,13},{13,9},{2,6},{6,2},{1... | collective-permute-start | bytes 49160 | tf_op jit(solution)/shard_map/ppermute | solution.py:327
  20.6 1.4 %collective-permute-start.3 = (bf16[64,128]{1,0:T(8,128)(2,1)S(1)}, bf16[64,128]{1,0:T(8,128)(2,1)S(1)}, u32[]{:S(2)}, u32[]{:S(2)}) collective-permute-start(bf16[64,128]{1,0:T(8,128)(2,1)S(1)} %get-tuple-element.15), channel_id=1, source_target_pairs={{4,8},{8,4},{5,9},{9,5},{6,10},{10,6},{7,11},{11,7},{20,24},{24,20... | collective-permute-start | bytes 49160 | tf_op jit(solution)/shard_map/ppermute | solution.py:327
  22.3 0.7 copy-start.6
  22.3 0.7 copy-start.7
where the time goes:
time: 72.2 us; the launch traced here: 71.3 us
  blocking collectives  35.9 us (50%)
  starting transfers between devices  16.3 us (23%)
  Pallas kernels  13.6 us (19%)
  local copies, waits for them, and re-layouts  3.84 us (5%)
  waiting for transfers between devices  1.03 us (1%)
    all_to_all x1, blocking collectives, on_device(): packs = lax.all_to_all(pack, BETA, 0, 0, tiled=True)  18.1 us
    all_to_all x1, blocking collectives, on_device(): parts = lax.all_to_all(part, ALPHA, 0, 0, tiled=True)  17.7 us
    pallas_call x4, Pallas kernels, call(): pl.pallas_call(kernel, out_shape=[shaped(shape, dtype) for shape, dtype i...  13.6 us
    all_to_all x1, starting transfers between devices, on_device(): targets = lax.all_to_all(tgt, ALPHA, 0, 0, tiled=True)  8.58 us
    ppermute x4, starting transfers between devices, swap(): return lax.ppermute(x, axes if len(axes) > 1 else axes[0], pairs)  7.74 us
    unnamed x16, local copies, waits for them, and re-layouts  3.84 us
  transfers between devices with their start and end apart: 5, of which 2 were waited for; matrix products, arithmetic and copies ran while one was open for 0% of the time, Pallas kernels for 0%

commit v1 on v0

--- a/solution.py
+++ b/solution.py
@@ -8,6 +8,7 @@
 from jax.experimental.pallas import tpu as pltpu
 from jax.sharding import Mesh
 from jax.sharding import PartitionSpec as P
+
 
 RHS = 16
 CX = 2
@@ -152,7 +153,10 @@
     return lax.axis_index("core") % 2, lax.axis_index("zh") % 2
 
 
-def prep_kernel(vol_ref, pts_ref, near_ref, tgt_ref, src_ref, order_ref, xe_ref, xo_ref, ye_ref, yo_ref, scr):
+def prep_kernel(vol_ref, pts_ref, near_ref, wts_ref, map_ref, tgt_ref, src_ref, wts_out, map_out,
+                xe_ref, xo_ref, ye_ref, yo_ref, order_ref, scr):
+    wts_out[...] = wts_ref[...]
+    map_out[...] = map_ref[...]
     v = vol_ref[...].reshape(CH * CX * CY, CZ).astype(bf16)
     row, col = iota((16, CZ), 0), iota((16, CZ), 1)
     pick = mask(((row == 0) & (col == CZ - 1)) | ((row == 1) & (col == 0)))
@@ -262,36 +266,37 @@
         c = order_ref[0, group * NT + q]
         return c // ROW, c % ROW
 
-    def dist(group, d_ref):
+    def dist(group, d_ref, q):
+        i, j = code(group, q)
+        d_ref[q] = jnp.dot(a_ref[j], tgt_ref[i], preferred_element_type=f32)
+
+    def add(group, g_ref, q):
+        i, j = code(group, q)
+        sum_ref[i] += jnp.dot(w_ref[j], g_ref[q], preferred_element_type=f32)
+
+    def values(d_ref, g_ref, q):
+        re, im = evaluate(d_ref[q])
+        g_ref[q, 0:PTS, :] = re
+        g_ref[q, PTS:, :] = im
+
+    for q in range(NT):
+        dist(0, d0, q)
+    g1[...] = jnp.zeros_like(g1)
+
+    def body(k, _):
         for q in range(NT):
-            i, j = code(group, q)
-            d_ref[q] = jnp.dot(a_ref[j], tgt_ref[i], preferred_element_type=f32)
-
-    def add(group, g_ref):
+            dist(2 * k + 1, d1, q)
+            values(d0, g0, q)
+            add(jnp.maximum(2 * k - 1, 0), g1, q)
         for q in range(NT):
-            i, j = code(group, q)
-            sum_ref[i] += jnp.dot(w_ref[j], g_ref[q], preferred_element_type=f32)
-
-    def values(d_ref, g_ref):
-        for q in range(NT):
-            re, im = evaluate(d_ref[q])
-            g_ref[q, 0:PTS, :] = re
-            g_ref[q, PTS:, :] = im
-
-    dist(0, d0)
-    g1[...] = jnp.zeros_like(g1)
-
-    def body(k, _):
-        dist(2 * k + 1, d1)
-        values(d0, g0)
-        add(jnp.maximum(2 * k - 1, 0), g1)
-        dist(2 * k + 2, d0)
-        values(d1, g1)
-        add(2 * k, g0)
+            dist(2 * k + 2, d0, q)
+            values(d1, g1, q)
+            add(2 * k, g0, q)
         return 0
 
     lax.fori_loop(0, pairs, body, 0)
-    add(jnp.maximum(2 * pairs - 1, 0), g1)
+    for q in range(NT):
+        add(jnp.maximum(2 * pairs - 1, 0), g1, q)
     out_ref[...] = sum_ref[...].astype(bf16)
 
 
@@ -308,16 +313,16 @@
     new_ref[...] = rel_ref[...] + spread.reshape(CH, CX, CY, CZ)
 
 
-def call(kernel, name, args, spaces, outs, scratch=(), keep=True):
-    args = [a if c == "s" else pltpu.with_memory_space_constraint(a, pltpu.VMEM) for a, c in zip(args, spaces)]
-    shaped = pltpu.VMEM if keep else jax.ShapeDtypeStruct
+def call(kernel, args, spaces, outs, kept, scratch=()):
+    args = [pltpu.with_memory_space_constraint(a, pltpu.VMEM) if c == "v" else a for a, c in zip(args, spaces)]
     return pl.pallas_call(
         kernel,
-        out_shape=[shaped(shape, dtype) for shape, dtype in outs],
+        out_shape=[
+            (pltpu.VMEM if c == "v" else jax.ShapeDtypeStruct)(shape, dtype) for (shape, dtype), c in zip(outs, kept)
+        ],
         in_specs=[pl.BlockSpec(memory_space=pltpu.SMEM if c == "s" else pltpu.VMEM) for c in spaces],
         out_specs=[pl.BlockSpec(memory_space=pltpu.VMEM)] * len(outs),
         scratch_shapes=[pltpu.VMEM(shape, dtype) for shape, dtype in scratch],
-        name=name,
     )(*args)
 
 
@@ -327,37 +332,39 @@
     return lax.ppermute(x, axes if len(axes) > 1 else axes[0], pairs)
 
 
-def on_device(volume, forcing, medium, points, weights, cell_map, near_list):
-    cells = cell_map[None, :]
+def sweep(volume, forcing, medium, points, weights, cell_map, near_list):
     face_x, face_y = (CH, CY, CZ), (CH * CX, CZ)
-    tgt, src, order, xe, xo, ye, yo = call(
+    tgt, src, wts, cells, xe, xo, ye, yo, order = call(
         prep_kernel,
-        "prep",
-        (volume, points, near_list),
-        "vvv",
-        [((NA, EXT, PTS), bf16), ((EXT, PTS), bf16), ((8, LIST), i32)]
-        + [(face, bf16) for face in (face_x, face_x, face_y, face_y)],
+        (volume, points, near_list, weights[None, :], cell_map[None, :]),
+        "hhhhh",
+        [((NA, EXT, PTS), bf16), ((EXT, PTS), bf16), ((1, PTS), f32), ((1, PTS), i32)]
+        + [(face, bf16) for face in (face_x, face_x, face_y, face_y)]
+        + [((8, LIST), i32)],
+        "vvvvvvvvh",
         [((EXT, PTS), f32)],
     )
+    grp = ("x", "zl", "core")
+    ye = swap(ye, ("zh",), 0)
+    yo = swap(yo, ("zh",), 1)
+    xo = swap(xo, grp, 1)
+    xe = swap(xe, grp, 0)
     targets = lax.all_to_all(tgt, ALPHA, 0, 0, tiled=True)
-    grp = ("x", "zl", "core")
-    ye, yo = swap(ye, ("zh",), 0), swap(yo, ("zh",), 1)
-    xo, xe = swap(xo, grp, 1), swap(xe, grp, 0)
     relaxed, pack = call(
         relax_kernel,
-        "relax",
-        (volume, forcing, medium, xe, xo, ye, yo, targets, weights[None, :], cells, src),
+        (volume, forcing, medium, xe, xo, ye, yo, targets, wts, cells, src),
         "v" * 11,
         [((CH, CX, CY, CZ), f32), ((NB, EXT + CH, PTS), bf16)],
+        "vv",
         [((16, CH * CX * CY), f32)],
     )
     packs = lax.all_to_all(pack, BETA, 0, 0, tiled=True)
     (part,) = call(
         pair_kernel,
-        "pairs",
         (order, packs, targets),
         "svv",
         [((NA, CH, PTS), bf16)],
+        "v",
         [
             ((NA, CH, PTS), f32),
             ((NB + 1, PTS, EXT), bf16),
@@ -370,12 +377,7 @@
     )
     parts = lax.all_to_all(part, ALPHA, 0, 0, tiled=True)
     new_volume, potential = call(
-        finish_kernel,
-        "finish",
-        (parts, relaxed, cells),
-        "vvv",
-        [((CH, CX, CY, CZ), f32), ((CH, PTS), f32)],
-        keep=False,
+        finish_kernel, (parts, relaxed, cells), "vvv", [((CH, CX, CY, CZ), f32), ((CH, PTS), f32)], "hh"
     )
     return new_volume, potential
 
@@ -384,7 +386,7 @@
     split = Mesh(np.asarray(mesh.devices).reshape([SIZES[a] for a in AXES]), AXES)
     grid = P(None, ("x", "zl", "core"), "zh", "y")
     return jax.shard_map(
-        on_device,
+        sweep,
         mesh=split,
         in_specs=(grid, grid, grid, P(None, AXES), P(AXES), P(AXES), P()),
         out_specs=(grid, P(None, AXES)),

time: 72.2 us -> 70.3 us (0.974)
  local copies, waits for them, and re-layouts: 3.84 us -> 0.01 us
  blocking collectives: 35.9 us -> 37.3 us
  Pallas kernels: 13.6 us -> 14.5 us
    unnamed x16 -> x6, local copies, waits for them, and re-layouts: 3.84 us -> 0.01 us
    all_to_all x2, blocking collectives: 35.9 us -> 37.3 us  [the longest x1 19.1 us: sweep(): parts = lax.all_to_all(part, ALPHA, 0, 0, tiled=True)]
    pallas_call x4, Pallas kernels: 13.6 us -> 14.5 us  [call(): pl.pallas_call(kernel, out_shape=[(pltpu.VMEM if c == 'v' else jax.ShapeD...]
where the time goes in v1:
time: 70.3 us; the launch traced here: 70 us
  blocking collectives  37.3 us (53%)
  starting transfers between devices  16.5 us (23%)
  Pallas kernels  14.5 us (21%)
  waiting for transfers between devices  1.03 us (1%)
    all_to_all x1, blocking collectives, sweep(): parts = lax.all_to_all(part, ALPHA, 0, 0, tiled=True)  19.1 us
    all_to_all x1, blocking collectives, sweep(): packs = lax.all_to_all(pack, BETA, 0, 0, tiled=True)  18.2 us
    pallas_call x4, Pallas kernels, call(): pl.pallas_call(kernel, out_shape=[(pltpu.VMEM if c == 'v' else jax.ShapeD...  14.5 us
    all_to_all x1, starting transfers between devices, sweep(): targets = lax.all_to_all(tgt, ALPHA, 0, 0, tiled=True)  8.71 us
    ppermute x4, starting transfers between devices, swap(): return lax.ppermute(x, axes if len(axes) > 1 else axes[0], pairs)  7.74 us
  transfers between devices with their start and end apart: 5, of which 2 were waited for; matrix products, arithmetic and copies ran while one was open for 0% of the time, Pallas kernels for 0%

profile of v1, /device:TPU:1, one launch (start us, length us, event | category | flops | bytes accessed | tf_op | source)
XLA Modules:
  0.0 70.0 jit_solution(10378253401451851796)
XLA Ops:
  0.6 0.0 copy-start.2
  0.6 2.5 %shard_map.86 = (bf16[32,32,128]{2,1,0:T(8,128)(2,1)}, bf16[32,128]{1,0:T(8,128)(2,1)S(1)}, f32[1,128]{1,0:T(1,128)S(1)}, s32[1,128]{1,0:T(1,128)S(1)}, bf16[32,...) custom-call(f32[32,2,8,128]{3,2,1,0:T(8,128)} %vol_ref.3, ...), custom_call_target="tpu_custom_call" | custom-call | tf_op jit(solution)/shard_map/pallas_call | solution.py:318
  3.1 0.0 copy-start
  3.1 0.0 copy-start.1
  3.1 8.7 %all-to-all-start = ((bf16[32,32,128]{2,1,0:T(8,128)(2,1)}), bf16[32,32,128]{2,1,0:T(8,128)(2,1)S(1)}, u32[]{:S(2)}, u32[]{:S(2)}) async-start(bf16[32,32,128]{2,1,0:T(8,128)(2,1)} %get-tuple-element.18), calls=%async_computation | async-start | bytes 524288 | tf_op jit(solution)/shard_map/all_to_all | solution.py:352
  11.9 0.3 collective-permute-start
  12.2 3.7 %collective-permute-start.1 = (bf16[32,8,128]{2,1,0:T(8,128)(2,1)S(1)}, bf16[32,8,128]{2,1,0:T(8,128)(2,1)S(1)}, u32[]{:S(2)}, u32[]{:S(2)}) collective-permute-start(bf16[32,8,128]{2,1,0:T(8,128)(2,1)S(1)} %get-tuple-element.15), channel_id=1, source_target_pairs={{16,32},{32,16},{48,64},{64,48},{80,96},{96,80},{112,128},{128,112... | collective-permute-start | bytes 196616 | tf_op jit(solution)/shard_map/ppermute | solution.py:332
  15.9 3.1 %collective-permute-start.2 = (bf16[64,128]{1,0:T(8,128)(2,1)S(1)}, bf16[64,128]{1,0:T(8,128)(2,1)S(1)}, u32[]{:S(2)}, u32[]{:S(2)}) collective-permute-start(bf16[64,128]{1,0:T(8,128)(2,1)S(1)} %get-tuple-element.16), channel_id=1, source_target_pairs={{0,4},{4,0},{8,12},{12,8},{1,5},{5,1},{9,13},{13,9},{2,6},{6,2},{1... | collective-permute-start | bytes 49160 | tf_op jit(solution)/shard_map/ppermute | solution.py:332
  19.0 0.7 collective-permute-start.3
  19.6 0.8 %collective-permute-done.2.ye_ref = bf16[64,128]{1,0:T(8,128)(2,1)S(1)} collective-permute-done((bf16[64,128]{1,0:T(8,128)(2,1)S(1)}, bf16[64,128]{1,0:T(8,128)(2,1)S(1)}, u32[]{:S(2)}, u32[]{:S(2)}) %collective-permute-start.2) | collective-permute-done | bytes 16416 | tf_op jit(solution)/shard_map/ppermute | solution.py:332
  20.4 0.0 collective-permute-done.3.yo_ref
  20.4 0.0 collective-permute-done.xe_ref
  20.4 0.0 collective-permute-done.1.xo_ref
  20.4 0.3 all-to-all-done.tgt_ref
  20.6 0.0 copy-done.2
  20.6 0.0 copy-done
  20.7 0.0 copy-done.1
  20.7 0.6 shard_map.87
  21.3 18.2 %all_to_all.15.pack_ref = bf16[8,64,128]{2,1,0:T(8,128)(2,1)S(1)} all-to-all(bf16[8,64,128]{2,1,0:T(8,128)(2,1)S(1)} %get-tuple-element.22), channel_id=1, replica_groups=mesh['x'=4,'zl'=2,'core'=2,'zh'=4,'y'=4] {'zl','zh'}, dimensions={0} | all-to-all | bytes 262144 | tf_op jit(solution)/shard_map/all_to_all | solution.py:361
  39.4 10.4 %shard_map.88 = bf16[32,32,128]{2,1,0:T(8,128)(2,1)S(1)} custom-call(s32[8,384]{1,0:T(8,128)} %get-tuple-element.13.order_ref, bf16[8,64,128]{2,1,0:T(8,128)(2,1)S(1)} %all_to_all.15.pack_ref, bf16[32,32,128]{2,1,0:T(8,128)(2,1)S(1)} %all-to-all-done.tgt_ref), custom_call_target="tpu_custom_call" | custom-call | tf_op jit(solution)/shard_map/pallas_call | solution.py:318
  49.8 19.1 %all_to_all.16.part_ref = bf16[32,32,128]{2,1,0:T(8,128)(2,1)S(1)} all-to-all(bf16[32,32,128]{2,1,0:T(8,128)(2,1)S(1)} %shard_map.88), channel_id=1, replica_groups=mesh['x'=4,'zl'=2,'core'=2,'zh'=4,'y'=4] {'x','core','y'}, dimensions={0} | all-to-all | bytes 524288 | tf_op jit(solution)/shard_map/all_to_all | solution.py:378
  69.0 1.0 %shard_map.89 = (f32[32,2,8,128]{3,2,1,0:T(8,128)}, f32[32,128]{1,0:T(8,128)}) custom-call(bf16[32,32,128]{2,1,0:T(8,128)(2,1)S(1)} %all_to_all.16.part_ref, f32[32,2,8,128]{3,2,1,0:T(8,128)S(1)} %get-tuple-element.23.rel_ref, s32[1,128]{1,0:T(1,128)S(1)} %get-tuple-element.20.map_ref), custom_call_target="tpu_custom_call" | custom-call | tf_op jit(solution)/shard_map/pallas_call | solution.py:318
Async XLA Ops:
  0.6 20.0 %copy-start.2 = (f32[2,2,8,128]{3,2,1,0:T(8,128)S(1)}, f32[2,2,8,128]{3,2,1,0:T(8,128)}, u32[]{:S(2)}) copy-start(f32[2,2,8,128]{3,2,1,0:T(8,128)} %med_ref.1) | copy-start | bytes 49156
  3.1 17.5 %copy-start = (f32[32,2,8,128]{3,2,1,0:T(8,128)S(1)}, f32[32,2,8,128]{3,2,1,0:T(8,128)}, u32[]{:S(2)}) copy-start(f32[32,2,8,128]{3,2,1,0:T(8,128)} %vol_ref.3) | copy-start | bytes 786436
  3.1 17.5 %copy-start.1 = (f32[32,2,8,128]{3,2,1,0:T(8,128)S(1)}, f32[32,2,8,128]{3,2,1,0:T(8,128)}, u32[]{:S(2)}) copy-start(f32[32,2,8,128]{3,2,1,0:T(8,128)} %forc_ref.1) | copy-start | bytes 786436
  3.1 17.5 %all-to-all-start = ((bf16[32,32,128]{2,1,0:T(8,128)(2,1)}), bf16[32,32,128]{2,1,0:T(8,128)(2,1)S(1)}, u32[]{:S(2)}, u32[]{:S(2)}) async-start(bf16[32,32,128]{2,1,0:T(8,128)(2,1)} %get-tuple-element.18), calls=%async_computation | async-start | bytes 524288 | tf_op jit(solution)/shard_map/all_to_all | solution.py:352
  11.9 8.5 %collective-permute-start = (bf16[32,8,128]{2,1,0:T(8,128)(2,1)S(1)}, bf16[32,8,128]{2,1,0:T(8,128)(2,1)S(1)}, u32[]{:S(2)}, u32[]{:S(2)}) collective-permute-start(bf16[32,8,128]{2,1,0:T(8,128)(2,1)S(1)} %get-tuple-element.14), channel_id=1, source_target_pairs={{0,16},{16,0},{32,48},{48,32},{64,80},{80,64},{96,112},{112,96},{1... | collective-permute-start | bytes 196616 | tf_op jit(solution)/shard_map/ppermute | solution.py:332
  12.2 8.2 %collective-permute-start.1 = (bf16[32,8,128]{2,1,0:T(8,128)(2,1)S(1)}, bf16[32,8,128]{2,1,0:T(8,128)(2,1)S(1)}, u32[]{:S(2)}, u32[]{:S(2)}) collective-permute-start(bf16[32,8,128]{2,1,0:T(8,128)(2,1)S(1)} %get-tuple-element.15), channel_id=1, source_target_pairs={{16,32},{32,16},{48,64},{64,48},{80,96},{96,80},{112,128},{128,112... | collective-permute-start | bytes 196616 | tf_op jit(solution)/shard_map/ppermute | solution.py:332
  15.9 4.5 %collective-permute-start.2 = (bf16[64,128]{1,0:T(8,128)(2,1)S(1)}, bf16[64,128]{1,0:T(8,128)(2,1)S(1)}, u32[]{:S(2)}, u32[]{:S(2)}) collective-permute-start(bf16[64,128]{1,0:T(8,128)(2,1)S(1)} %get-tuple-element.16), channel_id=1, source_target_pairs={{0,4},{4,0},{8,12},{12,8},{1,5},{5,1},{9,13},{13,9},{2,6},{6,2},{1... | collective-permute-start | bytes 49160 | tf_op jit(solution)/shard_map/ppermute | solution.py:332
  19.0 1.4 %collective-permute-start.3 = (bf16[64,128]{1,0:T(8,128)(2,1)S(1)}, bf16[64,128]{1,0:T(8,128)(2,1)S(1)}, u32[]{:S(2)}, u32[]{:S(2)}) collective-permute-start(bf16[64,128]{1,0:T(8,128)(2,1)S(1)} %get-tuple-element.17), channel_id=1, source_target_pairs={{4,8},{8,4},{5,9},{9,5},{6,10},{10,6},{7,11},{11,7},{20,24},{24,20... | collective-permute-start | bytes 49160 | tf_op jit(solution)/shard_map/ppermute | solution.py:332

commit v2 on v1

--- a/solution.py
+++ b/solution.py
@@ -30,17 +30,22 @@
 AXES = ("x", "zl", "core", "zh", "y")
 SIZES = dict(x=4, zl=2, core=2, zh=4, y=4)
 STRIDES = dict(x=64, zl=32, core=16, zh=4, y=1)
-ALPHA = ("x", "core", "y")
-BETA = ("zl", "zh")
+ALPHA = ("x", "y")
+BETA = ("zl", "core", "zh")
 NA = math.prod(SIZES[a] for a in ALPHA)
 NB = math.prod(SIZES[a] for a in BETA)
 TILES = NA * NB
 ROW = 64
 EXT = 32
-USED = 24
-STRIPS = CH * CX * CY // CZ
+HALO = 16
+BLOCK = 16
+SOURCE_ROWS = (0, 1, 2, 9, 0, 1, 2, 12, 3, 4, 5, 10, 3, 4, 5, 12, 0, 1, 2, 11, 6, 7, 8, 12)
+TARGET_ROWS = (0, 1, 2, 12, 3, 4, 5, 9, 0, 1, 2, 12, 3, 4, 5, 10, 6, 7, 8, 12, 0, 1, 2, 11)
 NT = 4
 LIST = 384
+
+GRP = ("x", "zl", "core")
+HALOS = tuple((f"halo_{n}{k}", axes) for n, axes in (("x", GRP), ("y", ("zh",)), ("z", ("y",))) for k in (0, 1))
 
 f32, bf16, i32 = jnp.float32, jnp.bfloat16, jnp.int32
 
@@ -101,28 +106,27 @@
     return condition.astype(f32).astype(bf16)
 
 
-def point_rows(pts, ends, scr, src_ref, tgt_ref):
+def point_rows(pts, scr, src_ref, tgt_ref):
     p = (pts - CENTRE) * TURN
     r = jnp.sum(p * p, axis=0, keepdims=True)
-    ah, am, al = split3(-2.0 * p)
-    bh, bm, bl = split3(p)
-    sh, sm, sl = split3(r)
-    th, tm, tl = split3(r + SOFTENING * TURN * TURN)
-    one = jnp.ones((1, PTS), f32)
-    scr[...] = jnp.zeros((EXT, PTS), f32)
-
-    def fill(*groups):
-        for n, (three, last) in enumerate(groups):
-            scr[4 * n : 4 * n + 3, :] = three
-            scr[4 * n + 3 : 4 * n + 4, :] = last
-
-    fill((ah, sh), (ah, one), (am, sm), (am, one), (ah, sl), (al, one))
+    scr[...] = jnp.ones((BLOCK, PTS), f32)
+
+    def fill(three, radius):
+        for n, (part, single) in enumerate(zip(split3(three), split3(radius))):
+            scr[3 * n : 3 * n + 3, :] = part
+            scr[9 + n : 10 + n, :] = single
+
+    fill(-2.0 * p, r)
     src_ref[...] = scr[...].astype(bf16)
-    fill((bh, one), (bm, th), (bh, one), (bm, tm), (bl, one), (bh, tl))
-    for k in range(STRIPS):
-        for end in range(2):
-            scr[USED + STRIPS * end + k : USED + STRIPS * end + k + 1, :] = ends[end : end + 1, CZ * k : CZ * (k + 1)]
+    fill(p, r + SOFTENING * TURN * TURN)
     tgt_ref[...] = jnp.broadcast_to(scr[...].astype(bf16)[None], tgt_ref.shape)
+
+
+def chooser(shape, along, rows):
+    place, wanted = iota(shape, along), jnp.full(shape, -1, i32)
+    for e, row in enumerate(rows):
+        wanted = jnp.where(place == e, row, wanted)
+    return mask(iota(shape, 1 - along) == wanted)
 
 
 def tile_order(near, order_ref):
@@ -150,37 +154,33 @@
 
 
 def parities():
-    return lax.axis_index("core") % 2, lax.axis_index("zh") % 2
+    return lax.axis_index("core") % 2, lax.axis_index("zh") % 2, lax.axis_index("y") % 2
 
 
 def prep_kernel(vol_ref, pts_ref, near_ref, wts_ref, map_ref, tgt_ref, src_ref, wts_out, map_out,
-                xe_ref, xo_ref, ye_ref, yo_ref, order_ref, scr):
+                xe_ref, xo_ref, ye_ref, yo_ref, ze_ref, zo_ref, order_ref, scr):
     wts_out[...] = wts_ref[...]
     map_out[...] = map_ref[...]
-    v = vol_ref[...].reshape(CH * CX * CY, CZ).astype(bf16)
-    row, col = iota((16, CZ), 0), iota((16, CZ), 1)
-    pick = mask(((row == 0) & (col == CZ - 1)) | ((row == 1) & (col == 0)))
-    point_rows(pts_ref[...], dot(pick, v, ((1,), (1,))), scr, src_ref, tgt_ref)
-    px, py = parities()
+    point_rows(pts_ref[...], scr, src_ref, tgt_ref)
+    px, py, pz = parities()
     xe_ref[...] = vol_ref[:, 1 - px].astype(bf16)
     xo_ref[...] = vol_ref[:, px].astype(bf16)
     low = vol_ref[:, :, 0, :].reshape(CH * CX, CZ).astype(bf16)
     high = vol_ref[:, :, CY - 1, :].reshape(CH * CX, CZ).astype(bf16)
     ye_ref[...] = jnp.where(py == 0, high, low)
     yo_ref[...] = jnp.where(py == 0, low, high)
+    v = vol_ref[...].reshape(CH * CX * CY, CZ).astype(bf16)
+    row, col = iota((HALO, CZ), 0), iota((HALO, CZ), 1)
+    up = mask((row == 0) & (col == CZ - 1))
+    down = mask((row == 1) & (col == 0))
+    ze_ref[...] = dot(jnp.where(pz == 0, up, down), v, ((1,), (1,))).astype(bf16)
+    zo_ref[...] = dot(jnp.where(pz == 0, down, up), v, ((1,), (1,))).astype(bf16)
     tile_order(mask(near_ref[...] != 0), order_ref)
 
 
-def joint_index(axes):
-    total = 0
-    for axis in axes:
-        total = total * SIZES[axis] + lax.axis_index(axis)
-    return total
-
-
-def relax_kernel(vol_ref, forc_ref, med_ref, xe_ref, xo_ref, ye_ref, yo_ref, tgt_ref,
-                 wts_ref, map_ref, src_ref, rel_ref, pack_ref, ends):
-    px, py = parities()
+def relax_kernel(vol_ref, forc_ref, med_ref, xe_ref, xo_ref, ye_ref, yo_ref, ze_ref, zo_ref,
+                 wts_ref, map_ref, src_ref, rel_ref, pack_ref):
+    px, py, _ = parities()
     v = vol_ref[...]
     xe, xo = xe_ref[...].astype(f32), xo_ref[...].astype(f32)
     xl, xh = jnp.where(px == 0, xo, xe), jnp.where(px == 0, xe, xo)
@@ -192,18 +192,9 @@
     by = jnp.where(row == 0, yl, pltpu.roll(v3, 1, 1)) + jnp.where(row == CY - 1, yh, pltpu.roll(v3, CY - 1, 1))
     v2 = v.reshape(CH * CX * CY, CZ)
     lane = iota(v2.shape, 1)
-    row, col = iota((16, CZ), 0), iota((16, CZ), 1)
+    row, col = iota((HALO, CZ), 0), iota((HALO, CZ), 1)
     place = mask(((row == 0) & (col == 0)) | ((row == 1) & (col == CZ - 1)))
-    own, along = joint_index(ALPHA), lax.axis_index("y")
-    half = EXT // 2
-    before = tgt_ref[jnp.maximum(own - 1, 0), half:, :].astype(f32) * (along > 0).astype(f32)
-    after = tgt_ref[jnp.minimum(own + 1, NA - 1), half:, :].astype(f32) * (along < SIZES["y"] - 1).astype(f32)
-    ends[...] = jnp.zeros_like(ends)
-    for k in range(STRIPS):
-        spot = USED - half + k
-        ends[0:1, CZ * k : CZ * (k + 1)] = before[spot : spot + 1]
-        ends[1:2, CZ * k : CZ * (k + 1)] = after[spot + STRIPS : spot + STRIPS + 1]
-    zhalo = ends[...].astype(bf16)
+    zhalo = (ze_ref[...].astype(f32) + zo_ref[...].astype(f32)).astype(bf16)
     bz = (
         jnp.where(lane == 0, 0.0, pltpu.roll(v2, 1, 1))
         + jnp.where(lane == CZ - 1, 0.0, pltpu.roll(v2, CZ - 1, 1))
@@ -231,8 +222,8 @@
     keep = (iota((CX * CY, PTS), 0) == cells // CZ).astype(f32)
     at = at.reshape(CH, CX * CY, PTS) * keep[None]
     traces = (jnp.sum(at, axis=1) * wts_ref[...]).astype(bf16)
-    pack_ref[:, 0:EXT, :] = jnp.broadcast_to(src_ref[...][None], (NB, EXT, PTS))
-    pack_ref[:, EXT:, :] = jnp.broadcast_to(traces[None], (NB, CH, PTS))
+    pack_ref[:, 0:BLOCK, :] = jnp.broadcast_to(src_ref[...][None], (NB, BLOCK, PTS))
+    pack_ref[:, BLOCK:, :] = jnp.broadcast_to(traces[None], (NB, CH, PTS))
 
 
 def evaluate(dist2):
@@ -251,11 +242,15 @@
     return (over - e * s2).astype(bf16), (e * c2).astype(bf16)
 
 
-def pair_kernel(order_ref, pack_ref, tgt_ref, out_ref, sum_ref, a_ref, w_ref, d0, d1, g0, g1):
+def pair_kernel(order_ref, pack_ref, tgt_ref, out_ref, sum_ref, a_ref, b_ref, w_ref, d0, d1, g0, g1):
     sum_ref[...] = jnp.zeros_like(sum_ref)
+    to_source = chooser((BLOCK, EXT), 1, SOURCE_ROWS)
+    to_target = chooser((EXT, BLOCK), 0, TARGET_ROWS)
+    for i in range(NA):
+        b_ref[i] = dot(to_target, tgt_ref[i], ((1,), (0,))).astype(bf16)
     for j in range(NB):
-        a_ref[j] = jnp.transpose(pack_ref[j, 0:EXT, :].astype(f32)).astype(bf16)
-        t = pack_ref[j, EXT:, :]
+        a_ref[j] = dot(pack_ref[j, 0:BLOCK, :], to_source, ((0,), (0,))).astype(bf16)
+        t = pack_ref[j, BLOCK:, :]
         w_ref[j, :, 0:PTS] = t
         w_ref[j, :, PTS:] = jnp.concatenate([-t[RHS:], t[:RHS]], 0)
     a_ref[NB] = a_ref[0]
@@ -268,7 +263,7 @@
 
     def dist(group, d_ref, q):
         i, j = code(group, q)
-        d_ref[q] = jnp.dot(a_ref[j], tgt_ref[i], preferred_element_type=f32)
+        d_ref[q] = jnp.dot(a_ref[j], b_ref[i], preferred_element_type=f32)
 
     def add(group, g_ref, q):
         i, j = code(group, q)
@@ -333,30 +328,27 @@
 
 
 def sweep(volume, forcing, medium, points, weights, cell_map, near_list):
-    face_x, face_y = (CH, CY, CZ), (CH * CX, CZ)
-    tgt, src, wts, cells, xe, xo, ye, yo, order = call(
+    face_x, face_y, face_z = (CH, CY, CZ), (CH * CX, CZ), (HALO, CH * CX * CY)
+    tgt, src, wts, cells, *faces, order = call(
         prep_kernel,
         (volume, points, near_list, weights[None, :], cell_map[None, :]),
         "hhhhh",
-        [((NA, EXT, PTS), bf16), ((EXT, PTS), bf16), ((1, PTS), f32), ((1, PTS), i32)]
-        + [(face, bf16) for face in (face_x, face_x, face_y, face_y)]
+        [((NA, BLOCK, PTS), bf16), ((BLOCK, PTS), bf16), ((1, PTS), f32), ((1, PTS), i32)]
+        + [(face, bf16) for face in (face_x, face_x, face_y, face_y, face_z, face_z)]
         + [((8, LIST), i32)],
-        "vvvvvvvvh",
-        [((EXT, PTS), f32)],
-    )
-    grp = ("x", "zl", "core")
-    ye = swap(ye, ("zh",), 0)
-    yo = swap(yo, ("zh",), 1)
-    xo = swap(xo, grp, 1)
-    xe = swap(xe, grp, 0)
+        "v" * 10 + "h",
+        [((BLOCK, PTS), f32)],
+    )
+    halos = []
+    for face, (name, axes) in zip(faces, HALOS):
+        halos.append(swap(face, axes, int(name[-1])))
     targets = lax.all_to_all(tgt, ALPHA, 0, 0, tiled=True)
     relaxed, pack = call(
         relax_kernel,
-        (volume, forcing, medium, xe, xo, ye, yo, targets, wts, cells, src),
-        "v" * 11,
-        [((CH, CX, CY, CZ), f32), ((NB, EXT + CH, PTS), bf16)],
+        (volume, forcing, medium, *halos, wts, cells, src),
+        "v" * 12,
+        [((CH, CX, CY, CZ), f32), ((NB, BLOCK + CH, PTS), bf16)],
         "vv",
-        [((16, CH * CX * CY), f32)],
     )
     packs = lax.all_to_all(pack, BETA, 0, 0, tiled=True)
     (part,) = call(
@@ -368,6 +360,7 @@
         [
             ((NA, CH, PTS), f32),
             ((NB + 1, PTS, EXT), bf16),
+            ((NA, EXT, PTS), bf16),
             ((NB + 1, CH, 2 * PTS), bf16),
             ((NT, PTS, PTS), f32),
             ((NT, PTS, PTS), f32),

time: 70.3 us -> 71.9 us (1.023)
  Pallas kernels: 14.5 us -> 15.8 us
  blocking collectives: 37.3 us -> 36.4 us
  starting transfers between devices: 16.5 us -> 17.4 us
    all_to_all x1, blocking collectives: 19.1 us -> 15.5 us  [sweep(): parts = lax.all_to_all(part, ALPHA, 0, 0, tiled=True)]
    ppermute x4 -> x6, starting transfers between devices: 7.74 us -> 10.9 us  [swap(): return lax.ppermute(x, axes if len(axes) > 1 else axes[0], pairs)]
    all_to_all x1, blocking collectives: 18.2 us -> 20.9 us  [sweep(): packs = lax.all_to_all(pack, BETA, 0, 0, tiled=True)]
    all_to_all x1, starting transfers between devices: 8.71 us -> 6.57 us  [sweep(): targets = lax.all_to_all(tgt, ALPHA, 0, 0, tiled=True)]
    pallas_call x4, Pallas kernels: 14.5 us -> 15.8 us  [call(): pl.pallas_call(kernel, out_shape=[(pltpu.VMEM if c == 'v' else jax.ShapeD...]
  transfers between devices with their start and end apart: 5 -> 7, of which waited for: 2 -> 1; matrix products, arithmetic and copies ran while one was open for 0% -> 0% of each run, Pallas kernels for 0% -> 1%
where the time goes in v2:
time: 71.9 us; the launch traced here: 71.5 us
  blocking collectives  36.4 us (51%)
  starting transfers between devices  17.4 us (24%)
  Pallas kernels  15.8 us (22%)
  waiting for transfers between devices  1.04 us (1%)
  between operations  0.75 us (1%)
    all_to_all x1, blocking collectives, sweep(): packs = lax.all_to_all(pack, BETA, 0, 0, tiled=True)  20.9 us
    pallas_call x4, Pallas kernels, call(): pl.pallas_call(kernel, out_shape=[(pltpu.VMEM if c == 'v' else jax.ShapeD...  15.8 us
    all_to_all x1, blocking collectives, sweep(): parts = lax.all_to_all(part, ALPHA, 0, 0, tiled=True)  15.5 us
    ppermute x6, starting transfers between devices, swap(): return lax.ppermute(x, axes if len(axes) > 1 else axes[0], pairs)  10.9 us
    all_to_all x1, starting transfers between devices, sweep(): targets = lax.all_to_all(tgt, ALPHA, 0, 0, tiled=True)  6.57 us
  transfers between devices with their start and end apart: 7, of which 1 were waited for; matrix products, arithmetic and copies ran while one was open for 0% of the time, Pallas kernels for 1%

profile of v2, /device:TPU:1, one launch (start us, length us, event | category | flops | bytes accessed | tf_op | source)
XLA Modules:
  0.0 71.5 jit_solution(16650918158280962646)
XLA Ops:
  0.6 0.0 copy-start
  0.6 0.0 copy-start.1
  0.7 2.5 %shard_map.86 = (bf16[16,16,128]{2,1,0:T(8,128)(2,1)}, bf16[16,128]{1,0:T(8,128)(2,1)S(1)}, f32[1,128]{1,0:T(1,128)S(1)}, s32[1,128]{1,0:T(1,128)S(1)}, bf16[32,...) custom-call(f32[32,2,8,128]{3,2,1,0:T(8,128)} %vol_ref.3, ...), custom_call_target="tpu_custom_call" | custom-call | tf_op jit(solution)/shard_map/pallas_call | solution.py:313
  3.1 3.2 %collective-permute-start = (bf16[32,8,128]{2,1,0:T(8,128)(2,1)S(1)}, bf16[32,8,128]{2,1,0:T(8,128)(2,1)S(1)}, u32[]{:S(2)}, u32[]{:S(2)}) collective-permute-start(bf16[32,8,128]{2,1,0:T(8,128)(2,1)S(1)} %get-tuple-element.16), channel_id=1, source_target_pairs={{0,16},{16,0},{32,48},{48,32},{64,80},{80,64},{96,112},{112,96},{1... | collective-permute-start | bytes 196616 | tf_op jit(solution)/shard_map/ppermute | solution.py:327
  6.3 1.9 %collective-permute-start.1 = (bf16[32,8,128]{2,1,0:T(8,128)(2,1)S(1)}, bf16[32,8,128]{2,1,0:T(8,128)(2,1)S(1)}, u32[]{:S(2)}, u32[]{:S(2)}) collective-permute-start(bf16[32,8,128]{2,1,0:T(8,128)(2,1)S(1)} %get-tuple-element.17), channel_id=1, source_target_pairs={{16,32},{32,16},{48,64},{64,48},{80,96},{96,80},{112,128},{128,112... | collective-permute-start | bytes 196616 | tf_op jit(solution)/shard_map/ppermute | solution.py:327
  8.3 0.0 copy-start.2
  8.3 6.6 %all-to-all-start.1 = ((bf16[16,16,128]{2,1,0:T(8,128)(2,1)}), bf16[16,16,128]{2,1,0:T(8,128)(2,1)S(1)}, u32[]{:S(2)}, u32[]{:S(2)}) async-start(bf16[16,16,128]{2,1,0:T(8,128)(2,1)} %get-tuple-element.26), calls=%async_computation.1 | async-start | bytes 131072 | tf_op jit(solution)/shard_map/all_to_all | solution.py:345
  14.9 3.1 %collective-permute-start.2 = (bf16[64,128]{1,0:T(8,128)(2,1)S(1)}, bf16[64,128]{1,0:T(8,128)(2,1)S(1)}, u32[]{:S(2)}, u32[]{:S(2)}) collective-permute-start(bf16[64,128]{1,0:T(8,128)(2,1)S(1)} %get-tuple-element.18), channel_id=1, source_target_pairs={{0,4},{4,0},{8,12},{12,8},{1,5},{5,1},{9,13},{13,9},{2,6},{6,2},{1... | collective-permute-start | bytes 49160 | tf_op jit(solution)/shard_map/ppermute | solution.py:327
  17.9 0.7 collective-permute-start.3
  18.6 1.4 %collective-permute-start.4 = (bf16[16,512]{1,0:T(8,128)(2,1)S(1)}, bf16[16,512]{1,0:T(8,128)(2,1)S(1)}, u32[]{:S(2)}, u32[]{:S(2)}) collective-permute-start(bf16[16,512]{1,0:T(8,128)(2,1)S(1)} %get-tuple-element.20), channel_id=1, source_target_pairs={{0,1},{1,0},{2,3},{3,2},{4,5},{5,4},{6,7},{7,6},{8,9},{9,8},{10,11... | collective-permute-start | bytes 49160 | tf_op jit(solution)/shard_map/ppermute | solution.py:327
  20.0 0.0 collective-permute-done.2.ye_ref
  20.0 0.7 collective-permute-start.5
  20.6 0.0 collective-permute-done.3.yo_ref
  20.6 1.0 %collective-permute-done.4.ze_ref = bf16[16,512]{1,0:T(8,128)(2,1)S(1)} collective-permute-done((bf16[16,512]{1,0:T(8,128)(2,1)S(1)}, bf16[16,512]{1,0:T(8,128)(2,1)S(1)}, u32[]{:S(2)}, u32[]{:S(2)}) %collective-permute-start.4) | collective-permute-done | bytes 16416 | tf_op jit(solution)/shard_map/ppermute | solution.py:327
  21.6 0.0 collective-permute-done.5.zo_ref
  21.7 0.0 collective-permute-done.xe_ref
  21.7 0.0 collective-permute-done.1.xo_ref
  21.7 0.0 copy-done
  21.7 0.0 copy-done.1
  21.7 0.0 copy-done.2
  21.7 0.6 shard_map.87
  22.3 0.0 all-to-all-done.1.tgt_ref
  22.3 20.9 %all_to_all.15.pack_ref = bf16[16,48,128]{2,1,0:T(8,128)(2,1)S(1)} all-to-all(bf16[16,48,128]{2,1,0:T(8,128)(2,1)S(1)} %get-tuple-element.25), channel_id=1, replica_groups=mesh['x'=4,'zl'=2,'core'=2,'zh'=4,'y'=4] {'zl','core','zh'}, dimensions={0} | all-to-all | bytes 393216 | tf_op jit(solution)/shard_map/all_to_all | solution.py:353
  43.2 11.7 %shard_map.88 = bf16[16,32,128]{2,1,0:T(8,128)(2,1)S(1)} custom-call(s32[8,384]{1,0:T(8,128)} %get-tuple-element.15.order_ref, bf16[16,48,128]{2,1,0:T(8,128)(2,1)S(1)} %all_to_all.15.pack_ref, bf16[16,16,128]{2,1,0:T(8,128)(2,1)S(1)} %all-to-all-done.1.tgt_ref), custom_call_target="tpu_custom_call" | custom-call | tf_op jit(solution)/shard_map/pallas_call | solution.py:313
  54.9 15.5 %all_to_all.16.part_ref = bf16[16,32,128]{2,1,0:T(8,128)(2,1)S(1)} all-to-all(bf16[16,32,128]{2,1,0:T(8,128)(2,1)S(1)} %shard_map.88), channel_id=1, replica_groups=mesh['x'=4,'zl'=2,'core'=2,'zh'=4,'y'=4] {'x','y'}, dimensions={0} | all-to-all | bytes 262144 | tf_op jit(solution)/shard_map/all_to_all | solution.py:371
  70.5 1.0 %shard_map.89 = (f32[32,2,8,128]{3,2,1,0:T(8,128)}, f32[32,128]{1,0:T(8,128)}) custom-call(bf16[16,32,128]{2,1,0:T(8,128)(2,1)S(1)} %all_to_all.16.part_ref, f32[32,2,8,128]{3,2,1,0:T(8,128)S(1)} %get-tuple-element.27.rel_ref, s32[1,128]{1,0:T(1,128)S(1)} %get-tuple-element.23.map_ref), custom_call_target="tpu_custom_call" | custom-call | tf_op jit(solution)/shard_map/pallas_call | solution.py:313
Async XLA Ops:
  0.6 21.0 %copy-start = (f32[32,2,8,128]{3,2,1,0:T(8,128)S(1)}, f32[32,2,8,128]{3,2,1,0:T(8,128)}, u32[]{:S(2)}) copy-start(f32[32,2,8,128]{3,2,1,0:T(8,128)} %vol_ref.3) | copy-start | bytes 786436
  0.6 21.0 %copy-start.1 = (f32[32,2,8,128]{3,2,1,0:T(8,128)S(1)}, f32[32,2,8,128]{3,2,1,0:T(8,128)}, u32[]{:S(2)}) copy-start(f32[32,2,8,128]{3,2,1,0:T(8,128)} %forc_ref.1) | copy-start | bytes 786436
  3.1 18.5 %collective-permute-start = (bf16[32,8,128]{2,1,0:T(8,128)(2,1)S(1)}, bf16[32,8,128]{2,1,0:T(8,128)(2,1)S(1)}, u32[]{:S(2)}, u32[]{:S(2)}) collective-permute-start(bf16[32,8,128]{2,1,0:T(8,128)(2,1)S(1)} %get-tuple-element.16), channel_id=1, source_target_pairs={{0,16},{16,0},{32,48},{48,32},{64,80},{80,64},{96,112},{112,96},{1... | collective-permute-start | bytes 196616 | tf_op jit(solution)/shard_map/ppermute | solution.py:327
  6.3 15.3 %collective-permute-start.1 = (bf16[32,8,128]{2,1,0:T(8,128)(2,1)S(1)}, bf16[32,8,128]{2,1,0:T(8,128)(2,1)S(1)}, u32[]{:S(2)}, u32[]{:S(2)}) collective-permute-start(bf16[32,8,128]{2,1,0:T(8,128)(2,1)S(1)} %get-tuple-element.17), channel_id=1, source_target_pairs={{16,32},{32,16},{48,64},{64,48},{80,96},{96,80},{112,128},{128,112... | collective-permute-start | bytes 196616 | tf_op jit(solution)/shard_map/ppermute | solution.py:327
  8.3 13.4 %copy-start.2 = (f32[2,2,8,128]{3,2,1,0:T(8,128)S(1)}, f32[2,2,8,128]{3,2,1,0:T(8,128)}, u32[]{:S(2)}) copy-start(f32[2,2,8,128]{3,2,1,0:T(8,128)} %med_ref.1) | copy-start | bytes 49156
  8.3 14.0 %all-to-all-start.1 = ((bf16[16,16,128]{2,1,0:T(8,128)(2,1)}), bf16[16,16,128]{2,1,0:T(8,128)(2,1)S(1)}, u32[]{:S(2)}, u32[]{:S(2)}) async-start(bf16[16,16,128]{2,1,0:T(8,128)(2,1)} %get-tuple-element.26), calls=%async_computation.1 | async-start | bytes 131072 | tf_op jit(solution)/shard_map/all_to_all | solution.py:345
  14.9 5.1 %collective-permute-start.2 = (bf16[64,128]{1,0:T(8,128)(2,1)S(1)}, bf16[64,128]{1,0:T(8,128)(2,1)S(1)}, u32[]{:S(2)}, u32[]{:S(2)}) collective-permute-start(bf16[64,128]{1,0:T(8,128)(2,1)S(1)} %get-tuple-element.18), channel_id=1, source_target_pairs={{0,4},{4,0},{8,12},{12,8},{1,5},{5,1},{9,13},{13,9},{2,6},{6,2},{1... | collective-permute-start | bytes 49160 | tf_op jit(solution)/shard_map/ppermute | solution.py:327
  17.9 2.7 %collective-permute-start.3 = (bf16[64,128]{1,0:T(8,128)(2,1)S(1)}, bf16[64,128]{1,0:T(8,128)(2,1)S(1)}, u32[]{:S(2)}, u32[]{:S(2)}) collective-permute-start(bf16[64,128]{1,0:T(8,128)(2,1)S(1)} %get-tuple-element.19), channel_id=1, source_target_pairs={{4,8},{8,4},{5,9},{9,5},{6,10},{10,6},{7,11},{11,7},{20,24},{24,20... | collective-permute-start | bytes 49160 | tf_op jit(solution)/shard_map/ppermute | solution.py:327
  18.6 3.1 %collective-permute-start.4 = (bf16[16,512]{1,0:T(8,128)(2,1)S(1)}, bf16[16,512]{1,0:T(8,128)(2,1)S(1)}, u32[]{:S(2)}, u32[]{:S(2)}) collective-permute-start(bf16[16,512]{1,0:T(8,128)(2,1)S(1)} %get-tuple-element.20), channel_id=1, source_target_pairs={{0,1},{1,0},{2,3},{3,2},{4,5},{5,4},{6,7},{7,6},{8,9},{9,8},{10,11... | collective-permute-start | bytes 49160 | tf_op jit(solution)/shard_map/ppermute | solution.py:327
  20.0 1.7 %collective-permute-start.5 = (bf16[16,512]{1,0:T(8,128)(2,1)S(1)}, bf16[16,512]{1,0:T(8,128)(2,1)S(1)}, u32[]{:S(2)}, u32[]{:S(2)}) collective-permute-start(bf16[16,512]{1,0:T(8,128)(2,1)S(1)} %get-tuple-element.21), channel_id=1, source_target_pairs={{1,2},{2,1},{5,6},{6,5},{9,10},{10,9},{13,14},{14,13},{17,18},{18,... | collective-permute-start | bytes 49160 | tf_op jit(solution)/shard_map/ppermute | solution.py:327

commit v3 on v2

--- a/solution.py
+++ b/solution.py
@@ -30,14 +30,16 @@
 AXES = ("x", "zl", "core", "zh", "y")
 SIZES = dict(x=4, zl=2, core=2, zh=4, y=4)
 STRIDES = dict(x=64, zl=32, core=16, zh=4, y=1)
-ALPHA = ("x", "y")
-BETA = ("zl", "core", "zh")
+ALPHA = ("core", "zh")
+BETA = ("x", "zl", "y")
 NA = math.prod(SIZES[a] for a in ALPHA)
 NB = math.prod(SIZES[a] for a in BETA)
 TILES = NA * NB
 ROW = 64
 EXT = 32
 HALO = 16
+FACE = CH * CY
+SIDE = CH * CX
 BLOCK = 16
 SOURCE_ROWS = (0, 1, 2, 9, 0, 1, 2, 12, 3, 4, 5, 10, 3, 4, 5, 12, 0, 1, 2, 11, 6, 7, 8, 12)
 TARGET_ROWS = (0, 1, 2, 12, 3, 4, 5, 9, 0, 1, 2, 12, 3, 4, 5, 10, 6, 7, 8, 12, 0, 1, 2, 11)
@@ -45,7 +47,6 @@
 LIST = 384
 
 GRP = ("x", "zl", "core")
-HALOS = tuple((f"halo_{n}{k}", axes) for n, axes in (("x", GRP), ("y", ("zh",)), ("z", ("y",))) for k in (0, 1))
 
 f32, bf16, i32 = jnp.float32, jnp.bfloat16, jnp.int32
 
@@ -119,7 +120,7 @@
     fill(-2.0 * p, r)
     src_ref[...] = scr[...].astype(bf16)
     fill(p, r + SOFTENING * TURN * TURN)
-    tgt_ref[...] = jnp.broadcast_to(scr[...].astype(bf16)[None], tgt_ref.shape)
+    tgt_ref[...] = scr[...].astype(bf16)
 
 
 def chooser(shape, along, rows):
@@ -129,8 +130,17 @@
     return mask(iota(shape, 1 - along) == wanted)
 
 
+def target_place(slot):
+    core, along = lax.axis_index("core"), lax.axis_index("zh")
+    core = jnp.where(slot % 2 == 1, 1 - core, core)
+    along = jnp.where(slot // 4 == 1, SIZES["zh"] - 1 - along, along)
+    along = jnp.where((slot // 2) % 2 == 1, along + 1 - 2 * (along % 2), along)
+    return core, along
+
+
 def tile_order(near, order_ref):
-    pick_rows = mask(iota((NA, 256), 1) == cluster_of(iota((NA, 256), 0), ALPHA) + own_part(BETA))
+    core, along = target_place(iota((NA, 256), 0))
+    pick_rows = mask(iota((NA, 256), 1) == core * STRIDES["core"] + along * STRIDES["zh"] + own_part(BETA))
     wide = iota((256, PTS), 1)
     pick_cols = mask((iota((256, PTS), 0) == cluster_of(wide, BETA) + own_part(ALPHA)) & (wide < NB))
     listed = dot(dot(pick_rows, near, ((1,), (0,))).astype(bf16), pick_cols, ((1,), (0,))).astype(bf16)
@@ -163,8 +173,9 @@
     map_out[...] = map_ref[...]
     point_rows(pts_ref[...], scr, src_ref, tgt_ref)
     px, py, pz = parities()
-    xe_ref[...] = vol_ref[:, 1 - px].astype(bf16)
-    xo_ref[...] = vol_ref[:, px].astype(bf16)
+    xe_ref[0:FACE, :] = vol_ref[:, 1 - px].reshape(FACE, CZ).astype(bf16)
+    xe_ref[FACE:, :] = tgt_ref[...]
+    xo_ref[...] = vol_ref[:, px].reshape(FACE, CZ).astype(bf16)
     low = vol_ref[:, :, 0, :].reshape(CH * CX, CZ).astype(bf16)
     high = vol_ref[:, :, CY - 1, :].reshape(CH * CX, CZ).astype(bf16)
     ye_ref[...] = jnp.where(py == 0, high, low)
@@ -178,16 +189,29 @@
     tile_order(mask(near_ref[...] != 0), order_ref)
 
 
+def near_kernel(face_ref, own_ref, core_ref, out_ref):
+    out_ref[0:SIDE, :] = face_ref[...]
+    out_ref[SIDE : SIDE + BLOCK, :] = own_ref[...]
+    out_ref[SIDE + BLOCK :, :] = core_ref[FACE:, :]
+
+
+def far_kernel(own_ref, core_ref, pair_ref, out_ref):
+    out_ref[0:BLOCK, :] = own_ref[...]
+    out_ref[BLOCK : 2 * BLOCK, :] = core_ref[FACE:, :]
+    out_ref[2 * BLOCK :, :] = pair_ref[SIDE:, :]
+
+
 def relax_kernel(vol_ref, forc_ref, med_ref, xe_ref, xo_ref, ye_ref, yo_ref, ze_ref, zo_ref,
                  wts_ref, map_ref, src_ref, rel_ref, pack_ref):
     px, py, _ = parities()
     v = vol_ref[...]
-    xe, xo = xe_ref[...].astype(f32), xo_ref[...].astype(f32)
+    xe = xe_ref[0:FACE, :].astype(f32).reshape(CH, CY, CZ)
+    xo = xo_ref[...].astype(f32).reshape(CH, CY, CZ)
     xl, xh = jnp.where(px == 0, xo, xe), jnp.where(px == 0, xe, xo)
     bx = jnp.stack([xl + v[:, 1], v[:, 0] + xh], axis=1)
     v3 = v.reshape(CH * CX, CY, CZ)
     row = iota(v3.shape, 1)
-    ye, yo = ye_ref[...].astype(f32), yo_ref[...].astype(f32)
+    ye, yo = ye_ref[0:SIDE, :].astype(f32), yo_ref[...].astype(f32)
     yl, yh = jnp.where(py == 0, yo, ye)[:, None, :], jnp.where(py == 0, ye, yo)[:, None, :]
     by = jnp.where(row == 0, yl, pltpu.roll(v3, 1, 1)) + jnp.where(row == CY - 1, yh, pltpu.roll(v3, CY - 1, 1))
     v2 = v.reshape(CH * CX * CY, CZ)
@@ -242,12 +266,14 @@
     return (over - e * s2).astype(bf16), (e * c2).astype(bf16)
 
 
-def pair_kernel(order_ref, pack_ref, tgt_ref, out_ref, sum_ref, a_ref, b_ref, w_ref, d0, d1, g0, g1):
+def pair_kernel(order_ref, pack_ref, near_ref, far_ref, out_ref, sum_ref, a_ref, b_ref, w_ref, d0, d1, g0, g1):
     sum_ref[...] = jnp.zeros_like(sum_ref)
     to_source = chooser((BLOCK, EXT), 1, SOURCE_ROWS)
     to_target = chooser((EXT, BLOCK), 0, TARGET_ROWS)
     for i in range(NA):
-        b_ref[i] = dot(to_target, tgt_ref[i], ((1,), (0,))).astype(bf16)
+        ref = near_ref if i < NA // 2 else far_ref
+        start = i % (NA // 2) * BLOCK
+        b_ref[i] = dot(to_target, ref[start : start + BLOCK, :], ((1,), (0,))).astype(bf16)
     for j in range(NB):
         a_ref[j] = dot(pack_ref[j, 0:BLOCK, :], to_source, ((0,), (0,))).astype(bf16)
         t = pack_ref[j, BLOCK:, :]
@@ -292,7 +318,9 @@
     lax.fori_loop(0, pairs, body, 0)
     for q in range(NT):
         add(jnp.maximum(2 * pairs - 1, 0), g1, q)
-    out_ref[...] = sum_ref[...].astype(bf16)
+    for i in range(NA):
+        core, along = target_place(jnp.int32(i))
+        out_ref[core * SIZES["zh"] + along] = sum_ref[i].astype(bf16)
 
 
 def finish_kernel(part_ref, rel_ref, map_ref, new_ref, pot_ref):
@@ -328,24 +356,30 @@
 
 
 def sweep(volume, forcing, medium, points, weights, cell_map, near_list):
-    face_x, face_y, face_z = (CH, CY, CZ), (CH * CX, CZ), (HALO, CH * CX * CY)
-    tgt, src, wts, cells, *faces, order = call(
+    tgt, src, wts, cells, xe, xo, ye, yo, ze, zo, order = call(
         prep_kernel,
         (volume, points, near_list, weights[None, :], cell_map[None, :]),
         "hhhhh",
-        [((NA, BLOCK, PTS), bf16), ((BLOCK, PTS), bf16), ((1, PTS), f32), ((1, PTS), i32)]
-        + [(face, bf16) for face in (face_x, face_x, face_y, face_y, face_z, face_z)]
+        [((BLOCK, PTS), bf16), ((BLOCK, PTS), bf16), ((1, PTS), f32), ((1, PTS), i32)]
+        + [((rows, CZ), bf16) for rows in (FACE + BLOCK, FACE, SIDE, SIDE)]
+        + [((HALO, CH * CX * CY), bf16)] * 2
         + [((8, LIST), i32)],
         "v" * 10 + "h",
         [((BLOCK, PTS), f32)],
     )
-    halos = []
-    for face, (name, axes) in zip(faces, HALOS):
-        halos.append(swap(face, axes, int(name[-1])))
-    targets = lax.all_to_all(tgt, ALPHA, 0, 0, tiled=True)
+    xe = swap(xe, GRP, 0)
+    xo = swap(xo, GRP, 1)
+    yo = swap(yo, ("zh",), 1)
+    ze = swap(ze, ("y",), 0)
+    zo = swap(zo, ("y",), 1)
+    (ye,) = call(near_kernel, (ye, tgt, xe), "vvv", [((SIDE + 2 * BLOCK, PTS), bf16)], "v")
+    ye = swap(ye, ("zh",), 0)
+    (quad,) = call(far_kernel, (tgt, xe, ye), "vvv", [((4 * BLOCK, PTS), bf16)], "v")
+    mirror = [(k, SIZES["zh"] - 1 - k) for k in range(SIZES["zh"])]
+    far = lax.ppermute(quad, "zh", mirror)
     relaxed, pack = call(
         relax_kernel,
-        (volume, forcing, medium, *halos, wts, cells, src),
+        (volume, forcing, medium, xe, xo, ye, yo, ze, zo, wts, cells, src),
         "v" * 12,
         [((CH, CX, CY, CZ), f32), ((NB, BLOCK + CH, PTS), bf16)],
         "vv",
@@ -353,8 +387,8 @@
     packs = lax.all_to_all(pack, BETA, 0, 0, tiled=True)
     (part,) = call(
         pair_kernel,
-        (order, packs, targets),
-        "svv",
+        (order, packs, quad, far),
+        "svvv",
         [((NA, CH, PTS), bf16)],
         "v",
         [

time: 71.9 us -> 66.3 us (0.922)
  blocking collectives: 36.4 us -> 20.5 us
  starting transfers between devices: 17.4 us -> 25.1 us
  waiting for transfers between devices: 1.04 us -> 4.82 us
  Pallas kernels: 15.8 us -> 14.5 us
    all_to_all x1 -> x0, blocking collectives: 20.9 us -> none  [sweep(): packs = lax.all_to_all(pack, BETA, 0, 0, tiled=True)]
    all_to_all x1, blocking collectives: 15.5 us -> 20.5 us  [sweep(): parts = lax.all_to_all(part, ALPHA, 0, 0, tiled=True)]
    ppermute x0 -> x1, starting transfers between devices: none -> 4.29 us  [sweep(): far = lax.ppermute(quad, 'zh', mirror)]
    ppermute x0 -> x1, waiting for transfers between devices: none -> 3.63 us  [sweep(): far = lax.ppermute(quad, 'zh', mirror)]
    all_to_all x1, starting transfers between devices: 6.57 us -> 10.1 us  [sweep(): packs = lax.all_to_all(pack, BETA, 0, 0, tiled=True)]
    pallas_call x4 -> x6, Pallas kernels: 15.8 us -> 14.5 us  [call(): pl.pallas_call(kernel, out_shape=[(pltpu.VMEM if c == 'v' else jax.ShapeD...]
  transfers between devices with their start and end apart: 7 -> 8, of which waited for: 1 -> 3; matrix products, arithmetic and copies ran while one was open for 0% -> 0% of each run, Pallas kernels for 1% -> 0%
where the time goes in v3:
time: 66.3 us; the launch traced here: 65.7 us
  starting transfers between devices  25.1 us (38%)
  blocking collectives  20.5 us (31%)
  Pallas kernels  14.5 us (22%)
  waiting for transfers between devices  4.82 us (7%)
  between operations  0.75 us (1%)
    all_to_all x1, blocking collectives, sweep(): parts = lax.all_to_all(part, ALPHA, 0, 0, tiled=True)  20.5 us
    pallas_call x6, Pallas kernels, call(): pl.pallas_call(kernel, out_shape=[(pltpu.VMEM if c == 'v' else jax.ShapeD...  14.5 us
    ppermute x6, starting transfers between devices, swap(): return lax.ppermute(x, axes if len(axes) > 1 else axes[0], pairs)  10.7 us
    all_to_all x1, starting transfers between devices, sweep(): packs = lax.all_to_all(pack, BETA, 0, 0, tiled=True)  10.1 us
    ppermute x1, starting transfers between devices, sweep(): far = lax.ppermute(quad, 'zh', mirror)  4.29 us
    ppermute x1, waiting for transfers between devices, sweep(): far = lax.ppermute(quad, 'zh', mirror)  3.63 us
  transfers between devices with their start and end apart: 8, of which 3 were waited for; matrix products, arithmetic and copies ran while one was open for 0% of the time, Pallas kernels for 0%

profile of v3, /device:TPU:1, one launch (start us, length us, event | category | flops | bytes accessed | tf_op | source)
XLA Modules:
  0.0 65.7 jit_solution(2989010317104784935)
XLA Ops:
  0.6 0.0 copy-start
  0.6 0.0 copy-start.1
  0.7 2.5 %shard_map.86 = (bf16[16,128]{1,0:T(8,128)(2,1)S(1)}, bf16[16,128]{1,0:T(8,128)(2,1)S(1)}, f32[1,128]{1,0:T(1,128)S(1)}, s32[1,128]{1,0:T(1,128)S(1)}, bf16[272,...) custom-call(f32[32,2,8,128]{3,2,1,0:T(8,128)} %vol_ref.3, ...), custom_call_target="tpu_custom_call" | custom-call | tf_op jit(solution)/shard_map/pallas_call | solution.py:341
  3.1 3.2 %collective-permute-start = (bf16[272,128]{1,0:T(8,128)(2,1)S(1)}, bf16[272,128]{1,0:T(8,128)(2,1)S(1)}, u32[]{:S(2)}, u32[]{:S(2)}) collective-permute-start(bf16[272,128]{1,0:T(8,128)(2,1)S(1)} %get-tuple-element.16), channel_id=1, source_target_pairs={{0,16},{16,0},{32,48},{48,32},{64,80},{80,64},{96,112},{112,96},{1... | collective-permute-start | bytes 208904 | tf_op jit(solution)/shard_map/ppermute | solution.py:355
  6.3 1.9 %collective-permute-start.1 = (bf16[256,128]{1,0:T(8,128)(2,1)S(1)}, bf16[256,128]{1,0:T(8,128)(2,1)S(1)}, u32[]{:S(2)}, u32[]{:S(2)}) collective-permute-start(bf16[256,128]{1,0:T(8,128)(2,1)S(1)} %get-tuple-element.17), channel_id=1, source_target_pairs={{16,32},{32,16},{48,64},{64,48},{80,96},{96,80},{112,128},{128,112... | collective-permute-start | bytes 196616 | tf_op jit(solution)/shard_map/ppermute | solution.py:355
  8.3 0.0 collective-permute-done.core_ref.xe_ref
  8.3 0.0 copy-start.2
  8.3 2.9 %collective-permute-start.2 = (bf16[96,128]{1,0:T(8,128)(2,1)S(1)}, bf16[96,128]{1,0:T(8,128)(2,1)S(1)}, u32[]{:S(2)}, u32[]{:S(2)}) collective-permute-start(bf16[96,128]{1,0:T(8,128)(2,1)S(1)} %shard_map.87), channel_id=1, source_target_pairs={{0,4},{4,0},{8,12},{12,8},{1,5},{5,1},{9,13},{13,9},{2,6},{6,2},{1... | collective-permute-start | bytes 73736 | tf_op jit(solution)/shard_map/ppermute | solution.py:355
  11.2 0.7 collective-permute-start.3
  11.8 1.4 %collective-permute-start.4 = (bf16[16,512]{1,0:T(8,128)(2,1)S(1)}, bf16[16,512]{1,0:T(8,128)(2,1)S(1)}, u32[]{:S(2)}, u32[]{:S(2)}) collective-permute-start(bf16[16,512]{1,0:T(8,128)(2,1)S(1)} %get-tuple-element.21), channel_id=1, source_target_pairs={{0,1},{1,0},{2,3},{3,2},{4,5},{5,4},{6,7},{7,6},{8,9},{9,8},{10,11... | collective-permute-start | bytes 49160 | tf_op jit(solution)/shard_map/ppermute | solution.py:355
  13.2 0.7 collective-permute-start.5
  13.9 0.0 collective-permute-done.3.yo_ref
  13.9 0.6 collective-permute-done.4.ze_ref
  14.5 0.0 collective-permute-done.5.zo_ref
  14.5 0.0 collective-permute-done.1.xo_ref
  14.5 0.0 collective-permute-done.2.ye_ref.pair_ref
  14.5 0.0 copy-done
  14.5 0.0 copy-done.1
  14.5 0.0 copy-done.2
  14.6 1.4 %shard_map.88 = (f32[32,2,8,128]{3,2,1,0:T(8,128)S(1)}, bf16[32,48,128]{2,1,0:T(8,128)(2,1)}) custom-call(f32[32,2,8,128]{3,2,1,0:T(8,128)S(1)} %copy-done, f32[32,2,8,128]{3,2,1,0:T(8,128)S(1)} %copy-done.1, f32[2,2,8,128]{3,2,1,0:T(8,128)S(1)} %copy-done.2, bf16[272,128]{1,0:T(8,128)(2,1)S(1)} %collective-permute-done.core_ref.xe_ref, ...), custom_call_target="tpu_custom_call" | custom-call | tf_op jit(solution)/shard_map/pallas_call | solution.py:341
  15.9 10.1 %all-to-all-start = ((bf16[32,48,128]{2,1,0:T(8,128)(2,1)}), bf16[32,48,128]{2,1,0:T(8,128)(2,1)S(1)}, u32[]{:S(2)}, u32[]{:S(2)}) async-start(bf16[32,48,128]{2,1,0:T(8,128)(2,1)} %get-tuple-element.26), calls=%async_computation | async-start | bytes 786432 | tf_op jit(solution)/shard_map/all_to_all | solution.py:387
  26.1 4.3 %collective-permute-start.6 = (bf16[64,128]{1,0:T(8,128)(2,1)S(1)}, bf16[64,128]{1,0:T(8,128)(2,1)S(1)}, u32[]{:S(2)}, u32[]{:S(2)}) collective-permute-start(bf16[64,128]{1,0:T(8,128)(2,1)S(1)} %shard_map.89.near_ref), channel_id=1, source_target_pairs={{0,12},{4,8},{8,4},{12,0},{1,13},{5,9},{9,5},{13,1},{2,14},{6,10},... | collective-permute-start | bytes 49160 | tf_op jit(solution)/shard_map/ppermute | solution.py:379
  30.3 3.6 %collective-permute-done.6.far_ref = bf16[64,128]{1,0:T(8,128)(2,1)S(1)} collective-permute-done((bf16[64,128]{1,0:T(8,128)(2,1)S(1)}, bf16[64,128]{1,0:T(8,128)(2,1)S(1)}, u32[]{:S(2)}, u32[]{:S(2)}) %collective-permute-start.6) | collective-permute-done | bytes 16416 | tf_op jit(solution)/shard_map/ppermute | solution.py:379
  34.0 0.6 all-to-all-done.pack_ref
  34.5 9.7 %shard_map.90 = bf16[8,32,128]{2,1,0:T(8,128)(2,1)S(1)} custom-call(s32[8,384]{1,0:T(8,128)} %get-tuple-element.15.order_ref, bf16[32,48,128]{2,1,0:T(8,128)(2,1)S(1)} %all-to-all-done.pack_ref, bf16[64,128]{1,0:T(8,128)(2,1)S(1)} %shard_map.89.near_ref, bf16[64,128]{1,0:T(8,128)(2,1)S(1)} %collective-permute-done.6.far_ref), custom_call_target="tpu_custom_call" | custom-call | tf_op jit(solution)/shard_map/pallas_call | solution.py:341
  44.2 20.5 %all_to_all.10.part_ref = bf16[8,32,128]{2,1,0:T(8,128)(2,1)S(1)} all-to-all(bf16[8,32,128]{2,1,0:T(8,128)(2,1)S(1)} %shard_map.90), channel_id=1, replica_groups=mesh['x'=4,'zl'=2,'core'=2,'zh'=4,'y'=4] {'core','zh'}, dimensions={0} | all-to-all | bytes 131072 | tf_op jit(solution)/shard_map/all_to_all | solution.py:405
  64.7 1.0 %shard_map.91 = (f32[32,2,8,128]{3,2,1,0:T(8,128)}, f32[32,128]{1,0:T(8,128)}) custom-call(bf16[8,32,128]{2,1,0:T(8,128)(2,1)S(1)} %all_to_all.10.part_ref, f32[32,2,8,128]{3,2,1,0:T(8,128)S(1)} %get-tuple-element.27.rel_ref, s32[1,128]{1,0:T(1,128)S(1)} %get-tuple-element.24.map_ref), custom_call_target="tpu_custom_call" | custom-call | tf_op jit(solution)/shard_map/pallas_call | solution.py:341
  (2 shorter events, 0.0 us)
Async XLA Ops:
  0.6 13.9 %copy-start = (f32[32,2,8,128]{3,2,1,0:T(8,128)S(1)}, f32[32,2,8,128]{3,2,1,0:T(8,128)}, u32[]{:S(2)}) copy-start(f32[32,2,8,128]{3,2,1,0:T(8,128)} %vol_ref.3) | copy-start | bytes 786436
  0.6 13.9 %copy-start.1 = (f32[32,2,8,128]{3,2,1,0:T(8,128)S(1)}, f32[32,2,8,128]{3,2,1,0:T(8,128)}, u32[]{:S(2)}) copy-start(f32[32,2,8,128]{3,2,1,0:T(8,128)} %forc_ref.1) | copy-start | bytes 786436
  3.1 5.1 %collective-permute-start = (bf16[272,128]{1,0:T(8,128)(2,1)S(1)}, bf16[272,128]{1,0:T(8,128)(2,1)S(1)}, u32[]{:S(2)}, u32[]{:S(2)}) collective-permute-start(bf16[272,128]{1,0:T(8,128)(2,1)S(1)} %get-tuple-element.16), channel_id=1, source_target_pairs={{0,16},{16,0},{32,48},{48,32},{64,80},{80,64},{96,112},{112,96},{1... | collective-permute-start | bytes 208904 | tf_op jit(solution)/shard_map/ppermute | solution.py:355
  6.3 8.2 %collective-permute-start.1 = (bf16[256,128]{1,0:T(8,128)(2,1)S(1)}, bf16[256,128]{1,0:T(8,128)(2,1)S(1)}, u32[]{:S(2)}, u32[]{:S(2)}) collective-permute-start(bf16[256,128]{1,0:T(8,128)(2,1)S(1)} %get-tuple-element.17), channel_id=1, source_target_pairs={{16,32},{32,16},{48,64},{64,48},{80,96},{96,80},{112,128},{128,112... | collective-permute-start | bytes 196616 | tf_op jit(solution)/shard_map/ppermute | solution.py:355
  8.3 6.3 %copy-start.2 = (f32[2,2,8,128]{3,2,1,0:T(8,128)S(1)}, f32[2,2,8,128]{3,2,1,0:T(8,128)}, u32[]{:S(2)}) copy-start(f32[2,2,8,128]{3,2,1,0:T(8,128)} %med_ref.1) | copy-start | bytes 49156
  8.3 6.2 %collective-permute-start.2 = (bf16[96,128]{1,0:T(8,128)(2,1)S(1)}, bf16[96,128]{1,0:T(8,128)(2,1)S(1)}, u32[]{:S(2)}, u32[]{:S(2)}) collective-permute-start(bf16[96,128]{1,0:T(8,128)(2,1)S(1)} %shard_map.87), channel_id=1, source_target_pairs={{0,4},{4,0},{8,12},{12,8},{1,5},{5,1},{9,13},{13,9},{2,6},{6,2},{1... | collective-permute-start | bytes 73736 | tf_op jit(solution)/shard_map/ppermute | solution.py:355
  11.2 2.7 %collective-permute-start.3 = (bf16[64,128]{1,0:T(8,128)(2,1)S(1)}, bf16[64,128]{1,0:T(8,128)(2,1)S(1)}, u32[]{:S(2)}, u32[]{:S(2)}) collective-permute-start(bf16[64,128]{1,0:T(8,128)(2,1)S(1)} %get-tuple-element.20), channel_id=1, source_target_pairs={{4,8},{8,4},{5,9},{9,5},{6,10},{10,6},{7,11},{11,7},{20,24},{24,20... | collective-permute-start | bytes 49160 | tf_op jit(solution)/shard_map/ppermute | solution.py:355
  11.8 2.7 %collective-permute-start.4 = (bf16[16,512]{1,0:T(8,128)(2,1)S(1)}, bf16[16,512]{1,0:T(8,128)(2,1)S(1)}, u32[]{:S(2)}, u32[]{:S(2)}) collective-permute-start(bf16[16,512]{1,0:T(8,128)(2,1)S(1)} %get-tuple-element.21), channel_id=1, source_target_pairs={{0,1},{1,0},{2,3},{3,2},{4,5},{5,4},{6,7},{7,6},{8,9},{9,8},{10,11... | collective-permute-start | bytes 49160 | tf_op jit(solution)/shard_map/ppermute | solution.py:355
  13.2 1.3 %collective-permute-start.5 = (bf16[16,512]{1,0:T(8,128)(2,1)S(1)}, bf16[16,512]{1,0:T(8,128)(2,1)S(1)}, u32[]{:S(2)}, u32[]{:S(2)}) collective-permute-start(bf16[16,512]{1,0:T(8,128)(2,1)S(1)} %get-tuple-element.22), channel_id=1, source_target_pairs={{1,2},{2,1},{5,6},{6,5},{9,10},{10,9},{13,14},{14,13},{17,18},{18,... | collective-permute-start | bytes 49160 | tf_op jit(solution)/shard_map/ppermute | solution.py:355
  15.9 18.6 %all-to-all-start = ((bf16[32,48,128]{2,1,0:T(8,128)(2,1)}), bf16[32,48,128]{2,1,0:T(8,128)(2,1)S(1)}, u32[]{:S(2)}, u32[]{:S(2)}) async-start(bf16[32,48,128]{2,1,0:T(8,128)(2,1)} %get-tuple-element.26), calls=%async_computation | async-start | bytes 786432 | tf_op jit(solution)/shard_map/all_to_all | solution.py:387
  26.1 7.9 %collective-permute-start.6 = (bf16[64,128]{1,0:T(8,128)(2,1)S(1)}, bf16[64,128]{1,0:T(8,128)(2,1)S(1)}, u32[]{:S(2)}, u32[]{:S(2)}) collective-permute-start(bf16[64,128]{1,0:T(8,128)(2,1)S(1)} %shard_map.89.near_ref), channel_id=1, source_target_pairs={{0,12},{4,8},{8,4},{12,0},{1,13},{5,9},{9,5},{13,1},{2,14},{6,10},... | collective-permute-start | bytes 49160 | tf_op jit(solution)/shard_map/ppermute | solution.py:379

commit v4 on v3

--- a/solution.py
+++ b/solution.py
@@ -47,6 +47,7 @@
 LIST = 384
 
 GRP = ("x", "zl", "core")
+
 
 f32, bf16, i32 = jnp.float32, jnp.bfloat16, jnp.int32
 
@@ -167,8 +168,13 @@
     return lax.axis_index("core") % 2, lax.axis_index("zh") % 2, lax.axis_index("y") % 2
 
 
-def prep_kernel(vol_ref, pts_ref, near_ref, wts_ref, map_ref, tgt_ref, src_ref, wts_out, map_out,
-                xe_ref, xo_ref, ye_ref, yo_ref, ze_ref, zo_ref, order_ref, scr):
+def order_kernel(near_ref, order_ref):
+    tile_order(mask(near_ref[...] != 0), order_ref)
+
+
+def prep_kernel(vol_ref, pts_ref, wts_ref, map_ref, tgt_ref, src_ref, vol_out, wts_out, map_out,
+                xe_ref, xo_ref, ye_ref, yo_ref, ze_ref, zo_ref, scr):
+    vol_out[...] = vol_ref[...]
     wts_out[...] = wts_ref[...]
     map_out[...] = map_ref[...]
     point_rows(pts_ref[...], scr, src_ref, tgt_ref)
@@ -186,7 +192,6 @@
     down = mask((row == 1) & (col == 0))
     ze_ref[...] = dot(jnp.where(pz == 0, up, down), v, ((1,), (1,))).astype(bf16)
     zo_ref[...] = dot(jnp.where(pz == 0, down, up), v, ((1,), (1,))).astype(bf16)
-    tile_order(mask(near_ref[...] != 0), order_ref)
 
 
 def near_kernel(face_ref, own_ref, core_ref, out_ref):
@@ -356,15 +361,14 @@
 
 
 def sweep(volume, forcing, medium, points, weights, cell_map, near_list):
-    tgt, src, wts, cells, xe, xo, ye, yo, ze, zo, order = call(
+    tgt, src, vol, wts, cells, xe, xo, ye, yo, ze, zo = call(
         prep_kernel,
-        (volume, points, near_list, weights[None, :], cell_map[None, :]),
-        "hhhhh",
-        [((BLOCK, PTS), bf16), ((BLOCK, PTS), bf16), ((1, PTS), f32), ((1, PTS), i32)]
+        (volume, points, weights[None, :], cell_map[None, :]),
+        "hhhh",
+        [((BLOCK, PTS), bf16), ((BLOCK, PTS), bf16), ((CH, CX, CY, CZ), f32), ((1, PTS), f32), ((1, PTS), i32)]
         + [((rows, CZ), bf16) for rows in (FACE + BLOCK, FACE, SIDE, SIDE)]
-        + [((HALO, CH * CX * CY), bf16)] * 2
-        + [((8, LIST), i32)],
-        "v" * 10 + "h",
+        + [((HALO, CH * CX * CY), bf16)] * 2,
+        "v" * 11,
         [((BLOCK, PTS), f32)],
     )
     xe = swap(xe, GRP, 0)
@@ -379,12 +383,13 @@
     far = lax.ppermute(quad, "zh", mirror)
     relaxed, pack = call(
         relax_kernel,
-        (volume, forcing, medium, xe, xo, ye, yo, ze, zo, wts, cells, src),
+        (vol, forcing, medium, xe, xo, ye, yo, ze, zo, wts, cells, src),
         "v" * 12,
         [((CH, CX, CY, CZ), f32), ((NB, BLOCK + CH, PTS), bf16)],
         "vv",
     )
     packs = lax.all_to_all(pack, BETA, 0, 0, tiled=True)
+    (order,) = call(order_kernel, (near_list,), "v", [((8, LIST), i32)], "h")
     (part,) = call(
         pair_kernel,
         (order, packs, quad, far),

time: 66.3 us -> 65.2 us (0.983)
  waiting for transfers between devices: 4.82 us -> 3.51 us
    ppermute x1, waiting for transfers between devices: 3.63 us -> 2.36 us  [sweep(): far = lax.ppermute(quad, 'zh', mirror)]
    pallas_call x6 -> x7, Pallas kernels: 14.5 us -> 14.6 us  [call(): pl.pallas_call(kernel, out_shape=[(pltpu.VMEM if c == 'v' else jax.ShapeD...]
  transfers between devices with their start and end apart: 8 -> 8, of which waited for: 3 -> 3; matrix products, arithmetic and copies ran while one was open for 0% -> 0% of each run, Pallas kernels for 0% -> 2%
where the time goes in v4:
time: 65.2 us; the launch traced here: 64.6 us
  starting transfers between devices  25.2 us (39%)
  blocking collectives  20.4 us (31%)
  Pallas kernels  14.6 us (22%)
  waiting for transfers between devices  3.51 us (5%)
  between operations  0.74 us (1%)
    all_to_all x1, blocking collectives, sweep(): parts = lax.all_to_all(part, ALPHA, 0, 0, tiled=True)  20.4 us
    pallas_call x7, Pallas kernels, call(): pl.pallas_call(kernel, out_shape=[(pltpu.VMEM if c == 'v' else jax.ShapeD...  14.6 us
    ppermute x6, starting transfers between devices, swap(): return lax.ppermute(x, axes if len(axes) > 1 else axes[0], pairs)  10.7 us
    all_to_all x1, starting transfers between devices, sweep(): packs = lax.all_to_all(pack, BETA, 0, 0, tiled=True)  10.2 us
    ppermute x1, starting transfers between devices, sweep(): far = lax.ppermute(quad, 'zh', mirror)  4.29 us
    ppermute x1, waiting for transfers between devices, sweep(): far = lax.ppermute(quad, 'zh', mirror)  2.36 us
  transfers between devices with their start and end apart: 8, of which 3 were waited for; matrix products, arithmetic and copies ran while one was open for 0% of the time, Pallas kernels for 2%

profile of v4, /device:TPU:1, one launch (start us, length us, event | category | flops | bytes accessed | tf_op | source)
XLA Modules:
  0.0 64.6 jit_solution(10824391115507388694)
XLA Ops:
  0.6 0.0 copy-start
  0.6 1.3 %shard_map.87 = (bf16[16,128]{1,0:T(8,128)(2,1)S(1)}, bf16[16,128]{1,0:T(8,128)(2,1)S(1)}, f32[32,2,8,128]{3,2,1,0:T(8,128)S(1)}, f32[1,128]{1,0:T(1,128)S(1)}, ...) custom-call(f32[32,2,8,128]{3,2,1,0:T(8,128)} %vol_ref.1, ...), custom_call_target="tpu_custom_call" | custom-call | tf_op jit(solution)/shard_map/pallas_call | solution.py:346
  1.9 3.2 %collective-permute-start = (bf16[272,128]{1,0:T(8,128)(2,1)S(1)}, bf16[272,128]{1,0:T(8,128)(2,1)S(1)}, u32[]{:S(2)}, u32[]{:S(2)}) collective-permute-start(bf16[272,128]{1,0:T(8,128)(2,1)S(1)} %get-tuple-element.16), channel_id=1, source_target_pairs={{0,16},{16,0},{32,48},{48,32},{64,80},{80,64},{96,112},{112,96},{1... | collective-permute-start | bytes 208904 | tf_op jit(solution)/shard_map/ppermute | solution.py:360
  5.1 1.9 %collective-permute-start.1 = (bf16[256,128]{1,0:T(8,128)(2,1)S(1)}, bf16[256,128]{1,0:T(8,128)(2,1)S(1)}, u32[]{:S(2)}, u32[]{:S(2)}) collective-permute-start(bf16[256,128]{1,0:T(8,128)(2,1)S(1)} %get-tuple-element.17), channel_id=1, source_target_pairs={{16,32},{32,16},{48,64},{64,48},{80,96},{96,80},{112,128},{128,112... | collective-permute-start | bytes 196616 | tf_op jit(solution)/shard_map/ppermute | solution.py:360
  7.1 0.0 collective-permute-done.core_ref.xe_ref
  7.1 0.0 copy-start.2
  7.1 2.9 %collective-permute-start.2 = (bf16[96,128]{1,0:T(8,128)(2,1)S(1)}, bf16[96,128]{1,0:T(8,128)(2,1)S(1)}, u32[]{:S(2)}, u32[]{:S(2)}) collective-permute-start(bf16[96,128]{1,0:T(8,128)(2,1)S(1)} %shard_map.88), channel_id=1, source_target_pairs={{0,4},{4,0},{8,12},{12,8},{1,5},{5,1},{9,13},{13,9},{2,6},{6,2},{1... | collective-permute-start | bytes 73736 | tf_op jit(solution)/shard_map/ppermute | solution.py:360
  10.0 0.7 %collective-permute-start.3 = (bf16[64,128]{1,0:T(8,128)(2,1)S(1)}, bf16[64,128]{1,0:T(8,128)(2,1)S(1)}, u32[]{:S(2)}, u32[]{:S(2)}) collective-permute-start(bf16[64,128]{1,0:T(8,128)(2,1)S(1)} %get-tuple-element.20), channel_id=1, source_target_pairs={{4,8},{8,4},{5,9},{9,5},{6,10},{10,6},{7,11},{11,7},{20,24},{24,20... | collective-permute-start | bytes 49160 | tf_op jit(solution)/shard_map/ppermute | solution.py:360
  10.7 1.4 %collective-permute-start.4 = (bf16[16,512]{1,0:T(8,128)(2,1)S(1)}, bf16[16,512]{1,0:T(8,128)(2,1)S(1)}, u32[]{:S(2)}, u32[]{:S(2)}) collective-permute-start(bf16[16,512]{1,0:T(8,128)(2,1)S(1)} %get-tuple-element.21), channel_id=1, source_target_pairs={{0,1},{1,0},{2,3},{3,2},{4,5},{5,4},{6,7},{7,6},{8,9},{9,8},{10,11... | collective-permute-start | bytes 49160 | tf_op jit(solution)/shard_map/ppermute | solution.py:360
  12.0 0.7 %collective-permute-start.5 = (bf16[16,512]{1,0:T(8,128)(2,1)S(1)}, bf16[16,512]{1,0:T(8,128)(2,1)S(1)}, u32[]{:S(2)}, u32[]{:S(2)}) collective-permute-start(bf16[16,512]{1,0:T(8,128)(2,1)S(1)} %get-tuple-element.22), channel_id=1, source_target_pairs={{1,2},{2,1},{5,6},{6,5},{9,10},{10,9},{13,14},{14,13},{17,18},{18,... | collective-permute-start | bytes 49160 | tf_op jit(solution)/shard_map/ppermute | solution.py:360
  12.7 0.0 collective-permute-done.3.yo_ref
  12.7 0.6 collective-permute-done.4.ze_ref
  13.3 0.0 collective-permute-done.5.zo_ref
  13.3 0.0 collective-permute-done.1.xo_ref
  13.3 0.0 collective-permute-done.2.ye_ref.pair_ref
  13.3 0.0 copy-done
  13.3 0.0 copy-done.2
  13.4 1.4 %shard_map.89 = (f32[32,2,8,128]{3,2,1,0:T(8,128)S(1)}, bf16[32,48,128]{2,1,0:T(8,128)(2,1)}) custom-call(f32[32,2,8,128]{3,2,1,0:T(8,128)S(1)} %get-tuple-element.15.vol_ref, f32[32,2,8,128]{3,2,1,0:T(8,128)S(1)} %copy-done, f32[2,2,8,128]{3,2,1,0:T(8,128)S(1)} %copy-done.2, bf16[272,128]{1,0:T(8,128)(2,1)S(1)} %collective-permute-done.core_ref.xe_ref, ...), custom_call_target="tpu_custom_call" | custom-call | tf_op jit(solution)/shard_map/pallas_call | solution.py:346
  14.8 0.0 copy-start.1
  14.8 10.2 %all-to-all-start = ((bf16[32,48,128]{2,1,0:T(8,128)(2,1)}), bf16[32,48,128]{2,1,0:T(8,128)(2,1)S(1)}, u32[]{:S(2)}, u32[]{:S(2)}) async-start(bf16[32,48,128]{2,1,0:T(8,128)(2,1)} %get-tuple-element.26), calls=%async_computation | async-start | bytes 786432 | tf_op jit(solution)/shard_map/all_to_all | solution.py:391
  25.0 4.3 %collective-permute-start.6 = (bf16[64,128]{1,0:T(8,128)(2,1)S(1)}, bf16[64,128]{1,0:T(8,128)(2,1)S(1)}, u32[]{:S(2)}, u32[]{:S(2)}) collective-permute-start(bf16[64,128]{1,0:T(8,128)(2,1)S(1)} %shard_map.90.near_ref), channel_id=1, source_target_pairs={{0,12},{4,8},{8,4},{12,0},{1,13},{5,9},{9,5},{13,1},{2,14},{6,10},... | collective-permute-start | bytes 49160 | tf_op jit(solution)/shard_map/ppermute | solution.py:383
  29.3 0.0 copy-done.1
  29.3 1.3 %shard_map.86.order_ref = s32[8,384]{1,0:T(8,128)} custom-call(s32[256,256]{1,0:T(8,128)S(1)} %copy-done.1), custom_call_target="tpu_custom_call" | custom-call | tf_op jit(solution)/shard_map/pallas_call | solution.py:346
  30.6 2.4 %collective-permute-done.6.far_ref = bf16[64,128]{1,0:T(8,128)(2,1)S(1)} collective-permute-done((bf16[64,128]{1,0:T(8,128)(2,1)S(1)}, bf16[64,128]{1,0:T(8,128)(2,1)S(1)}, u32[]{:S(2)}, u32[]{:S(2)}) %collective-permute-start.6) | collective-permute-done | bytes 16416 | tf_op jit(solution)/shard_map/ppermute | solution.py:383
  32.9 0.5 all-to-all-done.pack_ref
  33.5 9.7 %shard_map.91 = bf16[8,32,128]{2,1,0:T(8,128)(2,1)S(1)} custom-call(s32[8,384]{1,0:T(8,128)} %shard_map.86.order_ref, bf16[32,48,128]{2,1,0:T(8,128)(2,1)S(1)} %all-to-all-done.pack_ref, bf16[64,128]{1,0:T(8,128)(2,1)S(1)} %shard_map.90.near_ref, bf16[64,128]{1,0:T(8,128)(2,1)S(1)} %collective-permute-done.6.far_ref), custom_call_target="tpu_custom_call" | custom-call | tf_op jit(solution)/shard_map/pallas_call | solution.py:346
  43.1 20.4 %all_to_all.10.part_ref = bf16[8,32,128]{2,1,0:T(8,128)(2,1)S(1)} all-to-all(bf16[8,32,128]{2,1,0:T(8,128)(2,1)S(1)} %shard_map.91), channel_id=1, replica_groups=mesh['x'=4,'zl'=2,'core'=2,'zh'=4,'y'=4] {'core','zh'}, dimensions={0} | all-to-all | bytes 131072 | tf_op jit(solution)/shard_map/all_to_all | solution.py:410
  63.6 1.0 %shard_map.92 = (f32[32,2,8,128]{3,2,1,0:T(8,128)}, f32[32,128]{1,0:T(8,128)}) custom-call(bf16[8,32,128]{2,1,0:T(8,128)(2,1)S(1)} %all_to_all.10.part_ref, f32[32,2,8,128]{3,2,1,0:T(8,128)S(1)} %get-tuple-element.27.rel_ref, s32[1,128]{1,0:T(1,128)S(1)} %get-tuple-element.24.map_ref), custom_call_target="tpu_custom_call" | custom-call | tf_op jit(solution)/shard_map/pallas_call | solution.py:346
  (2 shorter events, 0.0 us)
Async XLA Ops:
  0.6 12.7 %copy-start = (f32[32,2,8,128]{3,2,1,0:T(8,128)S(1)}, f32[32,2,8,128]{3,2,1,0:T(8,128)}, u32[]{:S(2)}) copy-start(f32[32,2,8,128]{3,2,1,0:T(8,128)} %forc_ref.1) | copy-start | bytes 786436
  1.9 5.2 %collective-permute-start = (bf16[272,128]{1,0:T(8,128)(2,1)S(1)}, bf16[272,128]{1,0:T(8,128)(2,1)S(1)}, u32[]{:S(2)}, u32[]{:S(2)}) collective-permute-start(bf16[272,128]{1,0:T(8,128)(2,1)S(1)} %get-tuple-element.16), channel_id=1, source_target_pairs={{0,16},{16,0},{32,48},{48,32},{64,80},{80,64},{96,112},{112,96},{1... | collective-permute-start | bytes 208904 | tf_op jit(solution)/shard_map/ppermute | solution.py:360
  5.1 8.2 %collective-permute-start.1 = (bf16[256,128]{1,0:T(8,128)(2,1)S(1)}, bf16[256,128]{1,0:T(8,128)(2,1)S(1)}, u32[]{:S(2)}, u32[]{:S(2)}) collective-permute-start(bf16[256,128]{1,0:T(8,128)(2,1)S(1)} %get-tuple-element.17), channel_id=1, source_target_pairs={{16,32},{32,16},{48,64},{64,48},{80,96},{96,80},{112,128},{128,112... | collective-permute-start | bytes 196616 | tf_op jit(solution)/shard_map/ppermute | solution.py:360
  7.1 6.3 %copy-start.2 = (f32[2,2,8,128]{3,2,1,0:T(8,128)S(1)}, f32[2,2,8,128]{3,2,1,0:T(8,128)}, u32[]{:S(2)}) copy-start(f32[2,2,8,128]{3,2,1,0:T(8,128)} %med_ref.1) | copy-start | bytes 49156
  7.1 6.2 %collective-permute-start.2 = (bf16[96,128]{1,0:T(8,128)(2,1)S(1)}, bf16[96,128]{1,0:T(8,128)(2,1)S(1)}, u32[]{:S(2)}, u32[]{:S(2)}) collective-permute-start(bf16[96,128]{1,0:T(8,128)(2,1)S(1)} %shard_map.88), channel_id=1, source_target_pairs={{0,4},{4,0},{8,12},{12,8},{1,5},{5,1},{9,13},{13,9},{2,6},{6,2},{1... | collective-permute-start | bytes 73736 | tf_op jit(solution)/shard_map/ppermute | solution.py:360
  10.0 2.7 %collective-permute-start.3 = (bf16[64,128]{1,0:T(8,128)(2,1)S(1)}, bf16[64,128]{1,0:T(8,128)(2,1)S(1)}, u32[]{:S(2)}, u32[]{:S(2)}) collective-permute-start(bf16[64,128]{1,0:T(8,128)(2,1)S(1)} %get-tuple-element.20), channel_id=1, source_target_pairs={{4,8},{8,4},{5,9},{9,5},{6,10},{10,6},{7,11},{11,7},{20,24},{24,20... | collective-permute-start | bytes 49160 | tf_op jit(solution)/shard_map/ppermute | solution.py:360
  10.7 2.7 %collective-permute-start.4 = (bf16[16,512]{1,0:T(8,128)(2,1)S(1)}, bf16[16,512]{1,0:T(8,128)(2,1)S(1)}, u32[]{:S(2)}, u32[]{:S(2)}) collective-permute-start(bf16[16,512]{1,0:T(8,128)(2,1)S(1)} %get-tuple-element.21), channel_id=1, source_target_pairs={{0,1},{1,0},{2,3},{3,2},{4,5},{5,4},{6,7},{7,6},{8,9},{9,8},{10,11... | collective-permute-start | bytes 49160 | tf_op jit(solution)/shard_map/ppermute | solution.py:360
  12.0 1.3 %collective-permute-start.5 = (bf16[16,512]{1,0:T(8,128)(2,1)S(1)}, bf16[16,512]{1,0:T(8,128)(2,1)S(1)}, u32[]{:S(2)}, u32[]{:S(2)}) collective-permute-start(bf16[16,512]{1,0:T(8,128)(2,1)S(1)} %get-tuple-element.22), channel_id=1, source_target_pairs={{1,2},{2,1},{5,6},{6,5},{9,10},{10,9},{13,14},{14,13},{17,18},{18,... | collective-permute-start | bytes 49160 | tf_op jit(solution)/shard_map/ppermute | solution.py:360
  14.8 14.5 %copy-start.1 = (s32[256,256]{1,0:T(8,128)S(1)}, s32[256,256]{1,0:T(8,128)}, u32[]{:S(2)}) copy-start(s32[256,256]{1,0:T(8,128)} %near_ref.1) | copy-start | bytes 786436
  14.8 18.7 %all-to-all-start = ((bf16[32,48,128]{2,1,0:T(8,128)(2,1)}), bf16[32,48,128]{2,1,0:T(8,128)(2,1)S(1)}, u32[]{:S(2)}, u32[]{:S(2)}) async-start(bf16[32,48,128]{2,1,0:T(8,128)(2,1)} %get-tuple-element.26), calls=%async_computation | async-start | bytes 786432 | tf_op jit(solution)/shard_map/all_to_all | solution.py:391
  25.0 7.9 %collective-permute-start.6 = (bf16[64,128]{1,0:T(8,128)(2,1)S(1)}, bf16[64,128]{1,0:T(8,128)(2,1)S(1)}, u32[]{:S(2)}, u32[]{:S(2)}) collective-permute-start(bf16[64,128]{1,0:T(8,128)(2,1)S(1)} %shard_map.90.near_ref), channel_id=1, source_target_pairs={{0,12},{4,8},{8,4},{12,0},{1,13},{5,9},{9,5},{13,1},{2,14},{6,10},... | collective-permute-start | bytes 49160 | tf_op jit(solution)/shard_map/ppermute | solution.py:383

commit v5 on v4

--- a/solution.py
+++ b/solution.py
@@ -159,9 +159,9 @@
     found = dot(codes, hit, ((1,), (1,))).astype(i32)
     count = jnp.sum(flat, axis=1, keepdims=True).astype(i32)
     entry = jnp.where(iota((1, TILES), 1) < count, found[0:1] * ROW + found[1:2], NB)
-    order_ref[...] = jnp.full((8, LIST), NB, i32)
-    order_ref[0:1, 0:TILES] = entry
-    order_ref[1:2, 0:PTS] = jnp.broadcast_to(count, (1, PTS))
+    order_ref[:, 0:TILES] = entry
+    lane = iota((1, LIST - TILES), 1)
+    order_ref[:, TILES:] = jnp.where(lane == LIST - TILES - 1, count, NB)
 
 
 def parities():
@@ -286,11 +286,11 @@
         w_ref[j, :, PTS:] = jnp.concatenate([-t[RHS:], t[:RHS]], 0)
     a_ref[NB] = a_ref[0]
     w_ref[NB] = jnp.zeros((CH, 2 * PTS), bf16)
-    pairs = (order_ref[1, 0] + (2 * NT - 1)) // (2 * NT)
+    pairs = (order_ref[LIST - 1] + (2 * NT - 1)) // (2 * NT)
 
     def code(group, q):
-        c = order_ref[0, group * NT + q]
-        return c // ROW, c % ROW
+        c = order_ref[group * NT + q]
+        return c >> 6, c & (ROW - 1)
 
     def dist(group, d_ref, q):
         i, j = code(group, q)
@@ -389,7 +389,8 @@
         "vv",
     )
     packs = lax.all_to_all(pack, BETA, 0, 0, tiled=True)
-    (order,) = call(order_kernel, (near_list,), "v", [((8, LIST), i32)], "h")
+    (order,) = call(order_kernel, (near_list,), "v", [((1, LIST), i32)], "h")
+    order = order.reshape(LIST)
     (part,) = call(
         pair_kernel,
         (order, packs, quad, far),

time: 65.2 us -> 65.1 us (level)
  other arithmetic: 0 us -> 1.27 us
  waiting for transfers between devices: 3.51 us -> 2.28 us
    pallas_call x0 -> x1, other arithmetic: none -> 1.27 us  [call(): pl.pallas_call(kernel, out_shape=[(pltpu.VMEM if c == 'v' else jax.ShapeD...]
    ppermute x1, waiting for transfers between devices: 2.36 us -> 1.11 us  [sweep(): far = lax.ppermute(quad, 'zh', mirror)]
  transfers between devices with their start and end apart: 8 -> 8, of which waited for: 3 -> 3; matrix products, arithmetic and copies ran while one was open for 0% -> 2% of each run, Pallas kernels for 2% -> 2%
where the time goes in v5:
time: 65.1 us; the launch traced here: 64.5 us
  starting transfers between devices  25.3 us (39%)
  blocking collectives  20.4 us (31%)
  Pallas kernels  14.5 us (22%)
  waiting for transfers between devices  2.28 us (4%)
  other arithmetic  1.27 us (2%)
  between operations  0.74 us (1%)
    all_to_all x1, blocking collectives, sweep(): parts = lax.all_to_all(part, ALPHA, 0, 0, tiled=True)  20.4 us
    pallas_call x7, Pallas kernels, call(): pl.pallas_call(kernel, out_shape=[(pltpu.VMEM if c == 'v' else jax.ShapeD...  14.5 us
    ppermute x6, starting transfers between devices, swap(): return lax.ppermute(x, axes if len(axes) > 1 else axes[0], pairs)  10.7 us
    all_to_all x1, starting transfers between devices, sweep(): packs = lax.all_to_all(pack, BETA, 0, 0, tiled=True)  10.2 us
    ppermute x1, starting transfers between devices, sweep(): far = lax.ppermute(quad, 'zh', mirror)  4.29 us
  transfers between devices with their start and end apart: 8, of which 3 were waited for; matrix products, arithmetic and copies ran while one was open for 2% of the time, Pallas kernels for 2%

profile of v5, /device:TPU:1, one launch (start us, length us, event | category | flops | bytes accessed | tf_op | source)
XLA Modules:
  0.0 64.5 jit_solution(2911822220088181792)
XLA Ops:
  0.6 0.0 copy-start
  0.6 1.3 %shard_map.87 = (bf16[16,128]{1,0:T(8,128)(2,1)S(1)}, bf16[16,128]{1,0:T(8,128)(2,1)S(1)}, f32[32,2,8,128]{3,2,1,0:T(8,128)S(1)}, f32[1,128]{1,0:T(1,128)S(1)}, ...) custom-call(f32[32,2,8,128]{3,2,1,0:T(8,128)} %vol_ref.1, ...), custom_call_target="tpu_custom_call" | custom-call | tf_op jit(solution)/shard_map/pallas_call | solution.py:346
  1.9 3.2 %collective-permute-start = (bf16[272,128]{1,0:T(8,128)(2,1)S(1)}, bf16[272,128]{1,0:T(8,128)(2,1)S(1)}, u32[]{:S(2)}, u32[]{:S(2)}) collective-permute-start(bf16[272,128]{1,0:T(8,128)(2,1)S(1)} %get-tuple-element.16), channel_id=1, source_target_pairs={{0,16},{16,0},{32,48},{48,32},{64,80},{80,64},{96,112},{112,96},{1... | collective-permute-start | bytes 208904 | tf_op jit(solution)/shard_map/ppermute | solution.py:360
  5.1 1.9 %collective-permute-start.1 = (bf16[256,128]{1,0:T(8,128)(2,1)S(1)}, bf16[256,128]{1,0:T(8,128)(2,1)S(1)}, u32[]{:S(2)}, u32[]{:S(2)}) collective-permute-start(bf16[256,128]{1,0:T(8,128)(2,1)S(1)} %get-tuple-element.17), channel_id=1, source_target_pairs={{16,32},{32,16},{48,64},{64,48},{80,96},{96,80},{112,128},{128,112... | collective-permute-start | bytes 196616 | tf_op jit(solution)/shard_map/ppermute | solution.py:360
  7.1 0.0 collective-permute-done.core_ref.xe_ref
  7.1 0.0 copy-start.2
  7.1 2.9 %collective-permute-start.2 = (bf16[96,128]{1,0:T(8,128)(2,1)S(1)}, bf16[96,128]{1,0:T(8,128)(2,1)S(1)}, u32[]{:S(2)}, u32[]{:S(2)}) collective-permute-start(bf16[96,128]{1,0:T(8,128)(2,1)S(1)} %shard_map.88), channel_id=1, source_target_pairs={{0,4},{4,0},{8,12},{12,8},{1,5},{5,1},{9,13},{13,9},{2,6},{6,2},{1... | collective-permute-start | bytes 73736 | tf_op jit(solution)/shard_map/ppermute | solution.py:360
  10.0 0.7 %collective-permute-start.3 = (bf16[64,128]{1,0:T(8,128)(2,1)S(1)}, bf16[64,128]{1,0:T(8,128)(2,1)S(1)}, u32[]{:S(2)}, u32[]{:S(2)}) collective-permute-start(bf16[64,128]{1,0:T(8,128)(2,1)S(1)} %get-tuple-element.20), channel_id=1, source_target_pairs={{4,8},{8,4},{5,9},{9,5},{6,10},{10,6},{7,11},{11,7},{20,24},{24,20... | collective-permute-start | bytes 49160 | tf_op jit(solution)/shard_map/ppermute | solution.py:360
  10.7 1.4 %collective-permute-start.4 = (bf16[16,512]{1,0:T(8,128)(2,1)S(1)}, bf16[16,512]{1,0:T(8,128)(2,1)S(1)}, u32[]{:S(2)}, u32[]{:S(2)}) collective-permute-start(bf16[16,512]{1,0:T(8,128)(2,1)S(1)} %get-tuple-element.21), channel_id=1, source_target_pairs={{0,1},{1,0},{2,3},{3,2},{4,5},{5,4},{6,7},{7,6},{8,9},{9,8},{10,11... | collective-permute-start | bytes 49160 | tf_op jit(solution)/shard_map/ppermute | solution.py:360
  12.0 0.7 %collective-permute-start.5 = (bf16[16,512]{1,0:T(8,128)(2,1)S(1)}, bf16[16,512]{1,0:T(8,128)(2,1)S(1)}, u32[]{:S(2)}, u32[]{:S(2)}) collective-permute-start(bf16[16,512]{1,0:T(8,128)(2,1)S(1)} %get-tuple-element.22), channel_id=1, source_target_pairs={{1,2},{2,1},{5,6},{6,5},{9,10},{10,9},{13,14},{14,13},{17,18},{18,... | collective-permute-start | bytes 49160 | tf_op jit(solution)/shard_map/ppermute | solution.py:360
  12.7 0.0 collective-permute-done.3.yo_ref
  12.7 0.6 collective-permute-done.4.ze_ref
  13.3 0.0 collective-permute-done.5.zo_ref
  13.3 0.0 collective-permute-done.1.xo_ref
  13.3 0.0 collective-permute-done.2.ye_ref.pair_ref
  13.3 0.0 copy-done
  13.4 0.0 copy-done.2
  13.4 1.4 %shard_map.89 = (f32[32,2,8,128]{3,2,1,0:T(8,128)S(1)}, bf16[32,48,128]{2,1,0:T(8,128)(2,1)}) custom-call(f32[32,2,8,128]{3,2,1,0:T(8,128)S(1)} %get-tuple-element.15.vol_ref, f32[32,2,8,128]{3,2,1,0:T(8,128)S(1)} %copy-done, f32[2,2,8,128]{3,2,1,0:T(8,128)S(1)} %copy-done.2, bf16[272,128]{1,0:T(8,128)(2,1)S(1)} %collective-permute-done.core_ref.xe_ref, ...), custom_call_target="tpu_custom_call" | custom-call | tf_op jit(solution)/shard_map/pallas_call | solution.py:346
  14.7 0.0 copy-start.1
  14.7 10.2 %all-to-all-start = ((bf16[32,48,128]{2,1,0:T(8,128)(2,1)}), bf16[32,48,128]{2,1,0:T(8,128)(2,1)S(1)}, u32[]{:S(2)}, u32[]{:S(2)}) async-start(bf16[32,48,128]{2,1,0:T(8,128)(2,1)} %get-tuple-element.26), calls=%async_computation | async-start | bytes 786432 | tf_op jit(solution)/shard_map/all_to_all | solution.py:391
  25.0 4.3 %collective-permute-start.6 = (bf16[64,128]{1,0:T(8,128)(2,1)S(1)}, bf16[64,128]{1,0:T(8,128)(2,1)S(1)}, u32[]{:S(2)}, u32[]{:S(2)}) collective-permute-start(bf16[64,128]{1,0:T(8,128)(2,1)S(1)} %shard_map.90.near_ref), channel_id=1, source_target_pairs={{0,12},{4,8},{8,4},{12,0},{1,13},{5,9},{9,5},{13,1},{2,14},{6,10},... | collective-permute-start | bytes 49160 | tf_op jit(solution)/shard_map/ppermute | solution.py:383
  29.3 0.0 copy-done.1
  29.3 1.3 %shard_map.86 = s32[1,384]{1,0:T(1,128)} custom-call(s32[256,256]{1,0:T(8,128)S(1)} %copy-done.1), custom_call_target="tpu_custom_call" | custom-call | tf_op jit(solution)/shard_map/pallas_call | solution.py:346
  30.5 1.3 %reduce.order_ref = s32[384]{0:T(512)} reduce(s32[1,384]{1,0:T(1,128)} %shard_map.86, s32[]{:T(128)} %constant.6), dimensions={0}, to_apply=%pallas_call.51.reduce_sub_computation | reduce | bytes 3076 | tf_op jit(solution)/shard_map/pallas_call | solution.py:346
  31.8 1.1 %collective-permute-done.6.far_ref = bf16[64,128]{1,0:T(8,128)(2,1)S(1)} collective-permute-done((bf16[64,128]{1,0:T(8,128)(2,1)S(1)}, bf16[64,128]{1,0:T(8,128)(2,1)S(1)}, u32[]{:S(2)}, u32[]{:S(2)}) %collective-permute-start.6) | collective-permute-done | bytes 16416 | tf_op jit(solution)/shard_map/ppermute | solution.py:383
  32.9 0.5 all-to-all-done.pack_ref
  33.5 9.6 %shard_map.91 = bf16[8,32,128]{2,1,0:T(8,128)(2,1)S(1)} custom-call(s32[384]{0:T(512)} %reduce.order_ref, bf16[32,48,128]{2,1,0:T(8,128)(2,1)S(1)} %all-to-all-done.pack_ref, bf16[64,128]{1,0:T(8,128)(2,1)S(1)} %shard_map.90.near_ref, bf16[64,128]{1,0:T(8,128)(2,1)S(1)} %collective-permute-done.6.far_ref), custom_call_target="tpu_custom_call" | custom-call | tf_op jit(solution)/shard_map/pallas_call | solution.py:346
  43.1 20.4 %all_to_all.10.part_ref = bf16[8,32,128]{2,1,0:T(8,128)(2,1)S(1)} all-to-all(bf16[8,32,128]{2,1,0:T(8,128)(2,1)S(1)} %shard_map.91), channel_id=1, replica_groups=mesh['x'=4,'zl'=2,'core'=2,'zh'=4,'y'=4] {'core','zh'}, dimensions={0} | all-to-all | bytes 131072 | tf_op jit(solution)/shard_map/all_to_all | solution.py:411
  63.5 1.0 %shard_map.92 = (f32[32,2,8,128]{3,2,1,0:T(8,128)}, f32[32,128]{1,0:T(8,128)}) custom-call(bf16[8,32,128]{2,1,0:T(8,128)(2,1)S(1)} %all_to_all.10.part_ref, f32[32,2,8,128]{3,2,1,0:T(8,128)S(1)} %get-tuple-element.27.rel_ref, s32[1,128]{1,0:T(1,128)S(1)} %get-tuple-element.24.map_ref), custom_call_target="tpu_custom_call" | custom-call | tf_op jit(solution)/shard_map/pallas_call | solution.py:346
  (2 shorter events, 0.0 us)
Async XLA Ops:
  0.6 12.7 %copy-start = (f32[32,2,8,128]{3,2,1,0:T(8,128)S(1)}, f32[32,2,8,128]{3,2,1,0:T(8,128)}, u32[]{:S(2)}) copy-start(f32[32,2,8,128]{3,2,1,0:T(8,128)} %forc_ref.1) | copy-start | bytes 786436
  1.9 5.2 %collective-permute-start = (bf16[272,128]{1,0:T(8,128)(2,1)S(1)}, bf16[272,128]{1,0:T(8,128)(2,1)S(1)}, u32[]{:S(2)}, u32[]{:S(2)}) collective-permute-start(bf16[272,128]{1,0:T(8,128)(2,1)S(1)} %get-tuple-element.16), channel_id=1, source_target_pairs={{0,16},{16,0},{32,48},{48,32},{64,80},{80,64},{96,112},{112,96},{1... | collective-permute-start | bytes 208904 | tf_op jit(solution)/shard_map/ppermute | solution.py:360
  5.1 8.2 %collective-permute-start.1 = (bf16[256,128]{1,0:T(8,128)(2,1)S(1)}, bf16[256,128]{1,0:T(8,128)(2,1)S(1)}, u32[]{:S(2)}, u32[]{:S(2)}) collective-permute-start(bf16[256,128]{1,0:T(8,128)(2,1)S(1)} %get-tuple-element.17), channel_id=1, source_target_pairs={{16,32},{32,16},{48,64},{64,48},{80,96},{96,80},{112,128},{128,112... | collective-permute-start | bytes 196616 | tf_op jit(solution)/shard_map/ppermute | solution.py:360
  7.1 6.3 %copy-start.2 = (f32[2,2,8,128]{3,2,1,0:T(8,128)S(1)}, f32[2,2,8,128]{3,2,1,0:T(8,128)}, u32[]{:S(2)}) copy-start(f32[2,2,8,128]{3,2,1,0:T(8,128)} %med_ref.1) | copy-start | bytes 49156
  7.1 6.2 %collective-permute-start.2 = (bf16[96,128]{1,0:T(8,128)(2,1)S(1)}, bf16[96,128]{1,0:T(8,128)(2,1)S(1)}, u32[]{:S(2)}, u32[]{:S(2)}) collective-permute-start(bf16[96,128]{1,0:T(8,128)(2,1)S(1)} %shard_map.88), channel_id=1, source_target_pairs={{0,4},{4,0},{8,12},{12,8},{1,5},{5,1},{9,13},{13,9},{2,6},{6,2},{1... | collective-permute-start | bytes 73736 | tf_op jit(solution)/shard_map/ppermute | solution.py:360
  10.0 2.7 %collective-permute-start.3 = (bf16[64,128]{1,0:T(8,128)(2,1)S(1)}, bf16[64,128]{1,0:T(8,128)(2,1)S(1)}, u32[]{:S(2)}, u32[]{:S(2)}) collective-permute-start(bf16[64,128]{1,0:T(8,128)(2,1)S(1)} %get-tuple-element.20), channel_id=1, source_target_pairs={{4,8},{8,4},{5,9},{9,5},{6,10},{10,6},{7,11},{11,7},{20,24},{24,20... | collective-permute-start | bytes 49160 | tf_op jit(solution)/shard_map/ppermute | solution.py:360
  10.7 2.7 %collective-permute-start.4 = (bf16[16,512]{1,0:T(8,128)(2,1)S(1)}, bf16[16,512]{1,0:T(8,128)(2,1)S(1)}, u32[]{:S(2)}, u32[]{:S(2)}) collective-permute-start(bf16[16,512]{1,0:T(8,128)(2,1)S(1)} %get-tuple-element.21), channel_id=1, source_target_pairs={{0,1},{1,0},{2,3},{3,2},{4,5},{5,4},{6,7},{7,6},{8,9},{9,8},{10,11... | collective-permute-start | bytes 49160 | tf_op jit(solution)/shard_map/ppermute | solution.py:360
  12.0 1.3 %collective-permute-start.5 = (bf16[16,512]{1,0:T(8,128)(2,1)S(1)}, bf16[16,512]{1,0:T(8,128)(2,1)S(1)}, u32[]{:S(2)}, u32[]{:S(2)}) collective-permute-start(bf16[16,512]{1,0:T(8,128)(2,1)S(1)} %get-tuple-element.22), channel_id=1, source_target_pairs={{1,2},{2,1},{5,6},{6,5},{9,10},{10,9},{13,14},{14,13},{17,18},{18,... | collective-permute-start | bytes 49160 | tf_op jit(solution)/shard_map/ppermute | solution.py:360
  14.7 14.5 %copy-start.1 = (s32[256,256]{1,0:T(8,128)S(1)}, s32[256,256]{1,0:T(8,128)}, u32[]{:S(2)}) copy-start(s32[256,256]{1,0:T(8,128)} %near_ref.1) | copy-start | bytes 786436
  14.7 18.7 %all-to-all-start = ((bf16[32,48,128]{2,1,0:T(8,128)(2,1)}), bf16[32,48,128]{2,1,0:T(8,128)(2,1)S(1)}, u32[]{:S(2)}, u32[]{:S(2)}) async-start(bf16[32,48,128]{2,1,0:T(8,128)(2,1)} %get-tuple-element.26), calls=%async_computation | async-start | bytes 786432 | tf_op jit(solution)/shard_map/all_to_all | solution.py:391
  25.0 7.9 %collective-permute-start.6 = (bf16[64,128]{1,0:T(8,128)(2,1)S(1)}, bf16[64,128]{1,0:T(8,128)(2,1)S(1)}, u32[]{:S(2)}, u32[]{:S(2)}) collective-permute-start(bf16[64,128]{1,0:T(8,128)(2,1)S(1)} %shard_map.90.near_ref), channel_id=1, source_target_pairs={{0,12},{4,8},{8,4},{12,0},{1,13},{5,9},{9,5},{13,1},{2,14},{6,10},... | collective-permute-start | bytes 49160 | tf_op jit(solution)/shard_map/ppermute | solution.py:383
